TPU v7x, 256 devices: a whole 4x4x8 slice. The times are simulated.
256 devices in a mesh: space: 16 (over z, core), mode: 16 (over y, x).
Axes of the slice: x: 4, y: 4, z: 8, core: 2. Of those that a mesh axis runs over, the one named last changes fastest.
Arguments:
- guess: float32 [8192, 2048], P('space', 'mode'), may hold values from -6 to 6
- forcing: float32 [8192, 2048], P('space', 'mode'), may hold values from -6 to 6
- spatial_diag: bfloat16 [8192, 512], P('space'), may hold values from -0.25 to 0.25
- spatial_ghost: bfloat16 [8192, 256], P('space'), may hold values from -0.375 to 0.375
- ghost_rows: int32 [32, 128], P('space'), may hold values from 0 to 511, as said below
- chaos_vals: bfloat16 [128, 128, 128], P('mode'), may hold values from -0.25 to 0.25
- chaos_targets: int32 [16, 8], replicated, may hold values from 0 to 15, as said below
- chaos_count: int32 [16], replicated, may hold values from 1 to 8, as said below
- mean_inverse: bfloat16 [2048, 2048], replicated, may hold values from -0.125 to 0.125
Outputs:
- field: float32 [8192, 2048], P('space', 'mode')
Inputs may be any that keep to these rules, and one draw needn't show every extreme that they name: `ghost_rows`: each row holds 128 distinct node numbers, 0 and 511 among them. `chaos_targets`: the targets in a row are distinct and the first is the row's own chaos block. Only the first chaos_count[j] slots of row j are used; some row uses all 8 slots and some row only one.
All inputs are finite; a program needn't handle non-finite values.
Results may differ from a plain program's by a relative error of at most 0.0021.
Values may be sent and summed in bfloat16 or wider, within the bound.
A program may use at most 128 MiB of HBM per device.

v0:
```python
import jax
import jax.numpy as jnp
from jax import lax
from jax.sharding import Mesh
from jax.sharding import PartitionSpec as P

ITERS = 3
SPACE = ("space_0", "space_1")
MODE = ("mode_0", "mode_1")
SPACE_MODE = ("space_0", "space_1", "mode_0", "mode_1")


step_gain = 0.5


def with_halo(cells, sides, width):
    for axis, dim in sides:
        count = lax.axis_size(axis)
        ends = count - 1
        head = lax.slice_in_dim(cells, 0, width, axis=dim)
        tail = lax.slice_in_dim(cells, cells.shape[dim] - width, cells.shape[dim], axis=dim)
        cells = jnp.concatenate(
            [
                lax.ppermute(tail, axis, [(i, (i + 1) % count) for i in range(ends)]),
                cells,
                lax.ppermute(head, axis, [((i + 1) % count, i) for i in range(ends)]),
            ],
            axis=dim,
        )
    return cells


def one_axis_at_a_time(value, axes):
    for axis in axes:
        value = lax.psum(value, axis)
    return value


def shards(
    guess,
    forcing,
    spatial_diag,
    spatial_ghost,
    ghost_rows,
    chaos_vals,
    chaos_targets,
    chaos_count,
    mean_inverse,
):
    node_rows, local_modes = guess.shape
    ghost_width = ghost_rows.shape[1]
    block_width = chaos_vals.shape[1]
    list_slots = chaos_targets.shape[1]
    all_blocks = chaos_targets.shape[0]
    total_cells = node_rows * lax.axis_size(SPACE) * local_modes * lax.axis_size(MODE)
    slab_tables = lax.all_gather(chaos_vals, MODE, axis=0, tiled=True)
    slab_tables = slab_tables.reshape(all_blocks, list_slots, block_width, block_width)
    slot_used = jnp.arange(list_slots, dtype=jnp.int32)[None, :] < chaos_count[:, None]
    every_block = jnp.arange(all_blocks, dtype=jnp.int32)
    target_hits = (chaos_targets[:, :, None] == every_block[None, None, :]) & slot_used[:, :, None]
    target_hits = target_hits.astype(jnp.bfloat16)
    full_table = jnp.einsum(
        "jsba,jst->jatb", slab_tables, target_hits, preferred_element_type=jnp.float32
    )
    full_table = full_table.astype(jnp.bfloat16).reshape(
        all_blocks * block_width, all_blocks * block_width
    )
    field = guess
    for iteration in range(ITERS):
        field_bf = field.astype(jnp.bfloat16)
        lower_sent = field_bf[ghost_rows[0]]
        upper_sent = field_bf[ghost_rows[1]]
        padded = with_halo(
            jnp.concatenate([lower_sent, upper_sent], axis=0), ((SPACE, 0),), ghost_width
        )
        ghosts = jnp.concatenate([padded[:ghost_width], padded[3 * ghost_width :]], axis=0)
        spatial = jnp.dot(spatial_diag, field_bf, preferred_element_type=jnp.float32)
        spatial = spatial + jnp.dot(spatial_ghost, ghosts, preferred_element_type=jnp.float32)
        field_slab = lax.all_to_all(field_bf, MODE, split_axis=0, concat_axis=1, tiled=True)
        partial_slab = lax.all_to_all(
            forcing - spatial, MODE, split_axis=0, concat_axis=1, tiled=True
        )
        coupled_slab = jnp.dot(field_slab, full_table, preferred_element_type=jnp.float32)
        residual_slab = (partial_slab - coupled_slab).astype(jnp.bfloat16)
        update_slab = lax.dot_general(
            residual_slab,
            mean_inverse,
            (((1,), (1,)), ((), ())),
            preferred_element_type=jnp.float32,
        )
        update = lax.all_to_all(update_slab, MODE, split_axis=1, concat_axis=0, tiled=True)
        squares = one_axis_at_a_time(jnp.sum(update * update), SPACE_MODE)
        damping = step_gain / jnp.sqrt(squares / total_cells + 1e-06)
        field = field + damping * update
    return field


def solution(mesh):
    torus = Mesh(mesh.devices.reshape(8, 2, 4, 4), ("space_0", "space_1", "mode_0", "mode_1"))
    in_specs = (
        P(SPACE, MODE),
        P(SPACE, MODE),
        P(SPACE, None),
        P(SPACE, None),
        P(SPACE, None),
        P(MODE, None, None),
        P(),
        P(),
        P(),
    )
    out_specs = P(SPACE, MODE)
    return jax.shard_map(
        shards, mesh=torus, in_specs=in_specs, out_specs=out_specs, check_vma=False
    )
```

profile of v0, /device:TPU:1, one launch (start us, length us, event | category | flops | bytes accessed | tf_op | source)
XLA Modules:
  0.0 346.6 jit_solution(4169821131279760908)
XLA Ops:
  38.6 32.4 %all-gather.2.cloned.1.call-done = bf16[128,128,128]{2,1,0:T(8,128)(2,1)} async-done(((bf16[8,128,128]{2,1,0:T(8,128)(2,1)}), bf16[128,128,128]{2,1,0:T(8,128)(2,1)}) %all-gather.2.cloned.1.call-update) | async-done | bytes 4194320 | tf_op jit(solution)/shard_map/all_gather | solution.py:56
  71.0 7.5 %convert_bitcast_fusion = bf16[16,128,16,128]{1,2,3,0:T(8,128)(2,1)} fusion(bf16[16,8,128,128]{3,2,1,0:T(8,128)(2,1)} %bitcast.187, s32[16,8]{1,0:T(8,128)S(1)} %copy.36, pred[16,8]{1,0:T(8,128)(4,1)S(1)} %iota_compare_fusion.1), kind=kOutput, calls=%fused_computation.12 | convolution fusion | flops 71307264 | bytes 12583552 | tf_op jit(solution)/shard_map/jsba,jst->jatb/dot_general | solution.py:62
  78.5 13.3 %copy.38 = bf16[16,128,16,128]{3,2,1,0:T(8,128)(2,1)} copy(bf16[16,128,16,128]{1,2,3,0:T(8,128)(2,1)} %convert_bitcast_fusion) | data formatting | bytes 16777216 | tf_op jit(solution)/shard_map/convert_element_type | solution.py:65
  91.8 9.8 %convolution_bitcast_fusion.2 = f32[4,16,8,128]{3,2,1,0:T(8,128)S(1)} fusion(bf16[2048,2048]{1,0:T(8,128)(2,1)} %param.17, bf16[256,8,16,128]{3,2,1,0:T(8,128)(2,1)} %bitcast.184, f32[16,32,128]{2,1,0:T(8,128)S(1)} %all-to-all-done, bf16[16,32,128]{2,1,0:T(8,128)(2,1)S(1)} %all-to-all-done.1), kind=kOutput, calls=%fused_computation.32 | convolution fusion | flops 537001984 | bytes 17432576 | tf_op jit(solution)/shard_map/dot_general | solution.py:85
  101.7 12.3 %all_to_all.153 = f32[32,16,128]{2,0,1:T(8,128)S(1)} all-to-all(f32[32,16,128]{2,0,1:T(8,128)S(1)} %bitcast.190), channel_id=1, replica_groups=mesh['space_0'=8,'space_1'=2,'mode_0'=4,'mode_1'=4] {'mode_0','mode_1'}, dimensions={1} | all-to-all | bytes 524288 | tf_op jit(solution)/shard_map/all_to_all | solution.py:91
  114.7 14.3 %psum.84 = f32[]{:T(128)} all-reduce(f32[]{:T(128)} %multiply_reduce_fusion.2), channel_id=1, replica_groups=mesh['space_0'=8,'space_1'=2,'mode_0'=4,'mode_1'=4] {'space_0'}, use_global_device_ids=true, to_apply=%region_1.0 | all-reduce | flops 1 | bytes 8 | tf_op jit(solution)/shard_map/psum | solution.py:35
  129.0 8.7 %psum.85 = f32[]{:T(128)} all-reduce(f32[]{:T(128)} %psum.84), channel_id=1, replica_groups=mesh['space_0'=8,'space_1'=2,'mode_0'=4,'mode_1'=4] {'space_1'}, use_global_device_ids=true, to_apply=%region_2.0 | all-reduce | flops 1 | bytes 8 | tf_op jit(solution)/shard_map/psum | solution.py:35
  137.8 7.2 %psum.86 = f32[]{:T(128)} all-reduce(f32[]{:T(128)} %psum.85), channel_id=1, replica_groups=mesh['space_0'=8,'space_1'=2,'mode_0'=4,'mode_1'=4] {'mode_0'}, use_global_device_ids=true, to_apply=%region_3.0 | all-reduce | flops 1 | bytes 8 | tf_op jit(solution)/shard_map/psum | solution.py:35
  145.1 7.3 %psum.87 = f32[]{:T(128)} all-reduce(f32[]{:T(128)} %psum.86), channel_id=1, replica_groups=mesh['space_0'=8,'space_1'=2,'mode_0'=4,'mode_1'=4] {'mode_1'}, use_global_device_ids=true, to_apply=%region_4.0 | all-reduce | flops 1 | bytes 8 | tf_op jit(solution)/shard_map/psum | solution.py:35
  176.8 10.7 %all_to_all.154 = f32[16,32,128]{2,1,0:T(8,128)S(1)} all-to-all(f32[16,32,128]{2,1,0:T(8,128)S(1)} %bitcast.188), channel_id=1, replica_groups=mesh['space_0'=8,'space_1'=2,'mode_0'=4,'mode_1'=4] {'mode_0','mode_1'}, dimensions={0} | all-to-all | bytes 524288 | tf_op jit(solution)/shard_map/all_to_all | solution.py:80
  187.4 9.8 %convolution_bitcast_fusion.1 = f32[4,16,8,128]{3,2,1,0:T(8,128)S(1)} fusion(bf16[2048,2048]{1,0:T(8,128)(2,1)} %param.17, bf16[256,8,16,128]{3,2,1,0:T(8,128)(2,1)} %bitcast.185, f32[16,32,128]{2,1,0:T(8,128)S(1)} %all_to_all.154, bf16[16,32,128]{2,1,0:T(8,128)(2,1)S(1)} %all-to-all-done.4), kind=kOutput, calls=%fused_computation.28 | convolution fusion | flops 537001984 | bytes 17432576 | tf_op jit(solution)/shard_map/dot_general | solution.py:85
  197.2 10.5 %all_to_all.155 = f32[32,16,128]{2,0,1:T(8,128)S(1)} all-to-all(f32[32,16,128]{2,0,1:T(8,128)S(1)} %bitcast.191), channel_id=1, replica_groups=mesh['space_0'=8,'space_1'=2,'mode_0'=4,'mode_1'=4] {'mode_0','mode_1'}, dimensions={1} | all-to-all | bytes 524288 | tf_op jit(solution)/shard_map/all_to_all | solution.py:91
  208.4 12.9 %psum.88 = f32[]{:T(128)} all-reduce(f32[]{:T(128)} %multiply_reduce_fusion.1), channel_id=1, replica_groups=mesh['space_0'=8,'space_1'=2,'mode_0'=4,'mode_1'=4] {'space_0'}, use_global_device_ids=true, to_apply=%region_6.0 | all-reduce | flops 1 | bytes 8 | tf_op jit(solution)/shard_map/psum | solution.py:35
  221.3 9.3 %psum.89 = f32[]{:T(128)} all-reduce(f32[]{:T(128)} %psum.88), channel_id=1, replica_groups=mesh['space_0'=8,'space_1'=2,'mode_0'=4,'mode_1'=4] {'space_1'}, use_global_device_ids=true, to_apply=%region_7.0 | all-reduce | flops 1 | bytes 8 | tf_op jit(solution)/shard_map/psum | solution.py:35
  230.6 7.2 %psum.90 = f32[]{:T(128)} all-reduce(f32[]{:T(128)} %psum.89), channel_id=1, replica_groups=mesh['space_0'=8,'space_1'=2,'mode_0'=4,'mode_1'=4] {'mode_0'}, use_global_device_ids=true, to_apply=%region_8.0 | all-reduce | flops 1 | bytes 8 | tf_op jit(solution)/shard_map/psum | solution.py:35
  237.8 7.3 %psum.91 = f32[]{:T(128)} all-reduce(f32[]{:T(128)} %psum.90), channel_id=1, replica_groups=mesh['space_0'=8,'space_1'=2,'mode_0'=4,'mode_1'=4] {'mode_1'}, use_global_device_ids=true, to_apply=%region_9.0 | all-reduce | flops 1 | bytes 8 | tf_op jit(solution)/shard_map/psum | solution.py:35
  263.7 7.0 %all-to-all-done.7 = bf16[16,32,128]{2,1,0:T(8,128)(2,1)S(1)} async-done(((bf16[16,32,128]{2,1,0:T(8,128)(2,1)}), bf16[16,32,128]{2,1,0:T(8,128)(2,1)S(1)}, u32[]{:S(2)}, u32[]{:S(2)}) %all-to-all-start.7) | async-done | bytes 131104 | tf_op jit(solution)/shard_map/all_to_all | solution.py:79
  270.8 10.3 %all_to_all.156 = f32[16,32,128]{2,1,0:T(8,128)S(1)} all-to-all(f32[16,32,128]{2,1,0:T(8,128)S(1)} %bitcast.189), channel_id=1, replica_groups=mesh['space_0'=8,'space_1'=2,'mode_0'=4,'mode_1'=4] {'mode_0','mode_1'}, dimensions={0} | all-to-all | bytes 524288 | tf_op jit(solution)/shard_map/all_to_all | solution.py:80
  281.0 9.8 %convolution_bitcast_fusion = f32[4,16,8,128]{3,2,1,0:T(8,128)S(1)} fusion(bf16[2048,2048]{1,0:T(8,128)(2,1)} %param.17, bf16[256,8,16,128]{3,2,1,0:T(8,128)(2,1)} %bitcast.186, f32[16,32,128]{2,1,0:T(8,128)S(1)} %all_to_all.156, bf16[16,32,128]{2,1,0:T(8,128)(2,1)S(1)} %all-to-all-done.7), kind=kOutput, calls=%fused_computation.24 | convolution fusion | flops 537001984 | bytes 17432576 | tf_op jit(solution)/shard_map/dot_general | solution.py:85
  290.9 10.3 %all_to_all.157 = f32[32,16,128]{2,0,1:T(8,128)S(1)} all-to-all(f32[32,16,128]{2,0,1:T(8,128)S(1)} %bitcast.192), channel_id=1, replica_groups=mesh['space_0'=8,'space_1'=2,'mode_0'=4,'mode_1'=4] {'mode_0','mode_1'}, dimensions={1} | all-to-all | bytes 524288 | tf_op jit(solution)/shard_map/all_to_all | solution.py:91
  301.8 13.4 %psum.92 = f32[]{:T(128)} all-reduce(f32[]{:T(128)} %multiply_reduce_fusion), channel_id=1, replica_groups=mesh['space_0'=8,'space_1'=2,'mode_0'=4,'mode_1'=4] {'space_0'}, use_global_device_ids=true, to_apply=%region_11.0 | all-reduce | flops 1 | bytes 8 | tf_op jit(solution)/shard_map/psum | solution.py:35
  315.2 8.6 %psum.93 = f32[]{:T(128)} all-reduce(f32[]{:T(128)} %psum.92), channel_id=1, replica_groups=mesh['space_0'=8,'space_1'=2,'mode_0'=4,'mode_1'=4] {'space_1'}, use_global_device_ids=true, to_apply=%region_12.0 | all-reduce | flops 1 | bytes 8 | tf_op jit(solution)/shard_map/psum | solution.py:35
  323.8 7.2 %psum.94 = f32[]{:T(128)} all-reduce(f32[]{:T(128)} %psum.93), channel_id=1, replica_groups=mesh['space_0'=8,'space_1'=2,'mode_0'=4,'mode_1'=4] {'mode_0'}, use_global_device_ids=true, to_apply=%region_13.0 | all-reduce | flops 1 | bytes 8 | tf_op jit(solution)/shard_map/psum | solution.py:35
  331.0 7.3 %psum.95 = f32[]{:T(128)} all-reduce(f32[]{:T(128)} %psum.94), channel_id=1, replica_groups=mesh['space_0'=8,'space_1'=2,'mode_0'=4,'mode_1'=4] {'mode_1'}, use_global_device_ids=true, to_apply=%region_14.0 | all-reduce | flops 1 | bytes 8 | tf_op jit(solution)/shard_map/psum | solution.py:35
  (62 shorter events, 76.4 us)
Async XLA Ops:
  6.5 19.9 %copy-start = (bf16[512,512]{1,0:T(8,128)(2,1)S(1)}, bf16[512,512]{1,0:T(8,128)(2,1)}, u32[]{:S(2)}) copy-start(bf16[512,512]{1,0:T(8,128)(2,1)} %param.11) | copy-start | bytes 1572868
  6.5 64.4 %all-gather.2.cloned.1.call-start = ((), (), s32[]{:S(2)}) async-start(), calls=%async_computation.9 | async-start | bytes 4456448 | tf_op jit(solution)/shard_map/all_gather | solution.py:56
  11.2 17.9 %collective-permute-start.1 = (bf16[128,128]{1,0:T(8,128)(2,1)S(1)}, bf16[128,128]{1,0:T(8,128)(2,1)S(1)}, u32[]{:S(2)}, u32[]{:S(2)}) collective-permute-start(bf16[128,128]{1,0:T(8,128)(2,1)S(1)} %gather_fusion.1), channel_id=1, source_target_pairs={{16,0},{32,16},{48,32},{64,48},{80,64},{96,80},{112,96},{128,112},... | collective-permute-start | bytes 98312 | tf_op jit(solution)/shard_map/ppermute | solution.py:26
  17.9 11.2 %collective-permute-start = (bf16[128,128]{1,0:T(8,128)(2,1)S(1)}, bf16[128,128]{1,0:T(8,128)(2,1)S(1)}, u32[]{:S(2)}, u32[]{:S(2)}) collective-permute-start(bf16[128,128]{1,0:T(8,128)(2,1)S(1)} %gather_fusion), channel_id=1, source_target_pairs={{0,16},{16,32},{32,48},{48,64},{64,80},{80,96},{96,112},{112,128},... | collective-permute-start | bytes 98312 | tf_op jit(solution)/shard_map/ppermute | solution.py:24
  19.8 15.2 %all-to-all-start.1 = ((bf16[16,32,128]{2,1,0:T(8,128)(2,1)}), bf16[16,32,128]{2,1,0:T(8,128)(2,1)S(1)}, u32[]{:S(2)}, u32[]{:S(2)}) async-start(bf16[16,32,128]{2,1,0:T(8,128)(2,1)} %bitcast.11), calls=%async_computation.1 | async-start | bytes 262144 | tf_op jit(solution)/shard_map/all_to_all | solution.py:79
  35.0 56.8 %all-to-all-start = ((f32[16,32,128]{2,1,0:T(8,128)}), f32[16,32,128]{2,1,0:T(8,128)S(1)}, u32[]{:S(2)}, u32[]{:S(2)}) async-start(f32[16,32,128]{2,1,0:T(8,128)} %bitcast.5), calls=%async_computation | async-start | bytes 524288 | tf_op jit(solution)/shard_map/all_to_all | solution.py:80
  91.8 53.1 %copy-start.3 = (f32[512,128]{1,0:T(8,128)S(1)}, f32[512,128]{1,0:T(8,128)}, u32[]{:S(2)}) copy-start(f32[512,128]{1,0:T(8,128)} %param.10) | copy-start | bytes 786436
  91.8 61.3 %copy-start.1 = (f32[512,128]{1,0:T(8,128)S(1)}, f32[512,128]{1,0:T(8,128)}, u32[]{:S(2)}) copy-start(f32[512,128]{1,0:T(8,128)} %param.9) | copy-start | bytes 786436
  91.8 78.2 %copy-start.2 = (bf16[512,256]{1,0:T(8,128)(2,1)S(1)}, bf16[512,256]{1,0:T(8,128)(2,1)}, u32[]{:S(2)}) copy-start(bf16[512,256]{1,0:T(8,128)(2,1)} %param.12) | copy-start | bytes 786436
  157.0 13.0 %collective-permute-start.3 = (bf16[128,128]{1,0:T(8,128)(2,1)S(1)}, bf16[128,128]{1,0:T(8,128)(2,1)S(1)}, u32[]{:S(2)}, u32[]{:S(2)}) collective-permute-start(bf16[128,128]{1,0:T(8,128)(2,1)S(1)} %gather_fusion.3), channel_id=1, source_target_pairs={{16,0},{32,16},{48,32},{64,48},{80,64},{96,80},{112,96},{128,112},... | collective-permute-start | bytes 98312 | tf_op jit(solution)/shard_map/ppermute | solution.py:26
  163.3 6.7 %collective-permute-start.2 = (bf16[128,128]{1,0:T(8,128)(2,1)S(1)}, bf16[128,128]{1,0:T(8,128)(2,1)S(1)}, u32[]{:S(2)}, u32[]{:S(2)}) collective-permute-start(bf16[128,128]{1,0:T(8,128)(2,1)S(1)} %gather_fusion.2), channel_id=1, source_target_pairs={{0,16},{16,32},{32,48},{48,64},{64,80},{80,96},{96,112},{112,128},... | collective-permute-start | bytes 98312 | tf_op jit(solution)/shard_map/ppermute | solution.py:24
  166.4 10.3 %all-to-all-start.4 = ((bf16[16,32,128]{2,1,0:T(8,128)(2,1)}), bf16[16,32,128]{2,1,0:T(8,128)(2,1)S(1)}, u32[]{:S(2)}, u32[]{:S(2)}) async-start(bf16[16,32,128]{2,1,0:T(8,128)(2,1)} %bitcast.19), calls=%async_computation.4 | async-start | bytes 262144 | tf_op jit(solution)/shard_map/all_to_all | solution.py:79
  249.6 13.7 %collective-permute-start.5 = (bf16[128,128]{1,0:T(8,128)(2,1)S(1)}, bf16[128,128]{1,0:T(8,128)(2,1)S(1)}, u32[]{:S(2)}, u32[]{:S(2)}) collective-permute-start(bf16[128,128]{1,0:T(8,128)(2,1)S(1)} %gather_fusion.5), channel_id=1, source_target_pairs={{16,0},{32,16},{48,32},{64,48},{80,64},{96,80},{112,96},{128,112},... | collective-permute-start | bytes 98312 | tf_op jit(solution)/shard_map/ppermute | solution.py:26
  255.9 7.4 %collective-permute-start.4 = (bf16[128,128]{1,0:T(8,128)(2,1)S(1)}, bf16[128,128]{1,0:T(8,128)(2,1)S(1)}, u32[]{:S(2)}, u32[]{:S(2)}) collective-permute-start(bf16[128,128]{1,0:T(8,128)(2,1)S(1)} %gather_fusion.4), channel_id=1, source_target_pairs={{0,16},{16,32},{32,48},{48,64},{64,80},{80,96},{96,112},{112,128},... | collective-permute-start | bytes 98312 | tf_op jit(solution)/shard_map/ppermute | solution.py:24
  259.8 11.0 %all-to-all-start.7 = ((bf16[16,32,128]{2,1,0:T(8,128)(2,1)}), bf16[16,32,128]{2,1,0:T(8,128)(2,1)S(1)}, u32[]{:S(2)}, u32[]{:S(2)}) async-start(bf16[16,32,128]{2,1,0:T(8,128)(2,1)} %bitcast.26), calls=%async_computation.7 | async-start | bytes 262144 | tf_op jit(solution)/shard_map/all_to_all | solution.py:79
Sparse Core Ops, SparseCore 0:
  9.8 61.1 all-gather.1
where the time goes:
time: 351 us; the launch traced here: 347 us
  blocking collectives  165 us (47%)
  waiting for transfers between devices  50.5 us (14%)
  matrix products  42.9 us (12%)
  starting transfers between devices  41.3 us (12%)
  local copies, waits for them, and re-layouts  24 us (7%)
  between operations  15.8 us (5%)
  other arithmetic  7.31 us (2%)
    psum x12, blocking collectives, one_axis_at_a_time(): value = lax.psum(value, axis)  111 us
    all_to_all x3, blocking collectives, shards(): lax.all_to_all(update_slab, MODE, split_axis=1, concat_axis=0, tiled=True)  33.1 us
    all_gather x1, waiting for transfers between devices, shards(): slab_tables = lax.all_gather(chaos_vals, MODE, axis=0, tiled=True)  32.4 us
    dot_general x3, matrix products, shards(): lax.dot_general(residual_slab, mean_inverse, (((1,), (1,)), ((), ())), pr...  29.3 us
    all_to_all x2, blocking collectives, shards(): lax.all_to_all(forcing - spatial, MODE, split_axis=0, concat_axis=1, tile...  21 us
    ppermute x3, starting transfers between devices, with_halo(): lax.ppermute(head, axis, [((i + 1) % count, i) for i in range(ends)])  17.7 us
    all_to_all x3, waiting for transfers between devices, shards(): lax.all_to_all(field_bf, MODE, split_axis=0, concat_axis=1, tiled=True)  17.4 us
    all_to_all x3, starting transfers between devices, shards(): lax.all_to_all(field_bf, MODE, split_axis=0, concat_axis=1, tiled=True)  13.6 us
  transfers between devices with their start and end apart: 11, of which 4 were waited for; matrix products, arithmetic and copies ran while one was open for 10% of the time, Pallas kernels for 0%

commit v1 on v0

v1 whole, which is shorter than its diff:
```python
import functools

import jax
import jax.numpy as jnp
from jax import lax
from jax.experimental import pallas as pl
from jax.experimental.pallas import tpu as pltpu
from jax.sharding import PartitionSpec as P

STEPS = 3
step_gain = 0.5
BF = jnp.bfloat16
F32 = jnp.float32
A_F, A_SF, A_G, A_GLO, A_SG, A_S2F, A_S2G = range(7)
PLACE = {A_F: (0, 0), A_SF: (0, 1), A_S2F: (0, 2), A_G: (1, 0), A_SG: (1, 1), A_S2G: (1, 2), A_GLO: (1, 3)}


def dot(a, b):
    return jnp.dot(a, b, preferred_element_type=F32)


def split(x):
    high = x.astype(BF)
    return high, (x - high.astype(F32)).astype(BF)


def kernel(
    sizes,
    f_ref, force_ref, sd_ref, sg_ref, rows_ref, vals_ref, inv_ref, m_hbm,
    o_ref,
    m_ref, c_ref, cv_ref, oh_ref, arr_ref, gsend_ref, ghost_ref,
    got_ref, x_ref, add_ref, v_ref, back_src, back_got, gram_src, gram_got,
    m_sem, l_sem, gh_send, gh_recv, a_send, a_recv, c_send, c_recv, b_send, b_recv, r_send, r_recv,
):
    ns, nm, nx, slab, ghost, width, slots = sizes
    ny = nm // nx
    half = slots // 2
    nodes = f_ref.shape[0]
    s, m = lax.axis_index("space"), lax.axis_index("mode")
    c = s % 2
    y, x = m // nx, m % nx
    mesh = pl.DeviceIdType.MESH

    def send(src, dst, ssem, rsem, to_s, to_m):
        cp = pltpu.make_async_remote_copy(
            src_ref=src, dst_ref=dst, send_sem=ssem, recv_sem=rsem,
            device_id={"space": to_s, "mode": to_m}, device_id_type=mesh,
        )
        cp.start()

    def arrived(dst, rsem):
        pltpu.make_async_remote_copy(
            src_ref=dst, dst_ref=dst, send_sem=rsem, recv_sem=rsem,
            device_id={"space": s, "mode": m}, device_id_type=mesh,
        ).wait_recv()

    def sent(src, ssem):
        pltpu.make_async_remote_copy(
            src_ref=src, dst_ref=src, send_sem=ssem, recv_sem=ssem,
            device_id={"space": s, "mode": m}, device_id_type=mesh,
        ).wait_send()

    barrier = pltpu.get_barrier_semaphore()

    def greet_mode(k, _):
        pl.semaphore_signal(barrier, inc=1, device_id={"space": s, "mode": (m + k) % nm}, device_id_type=mesh)
        return 0

    def greet_space(k, _):
        pl.semaphore_signal(barrier, inc=1, device_id={"space": (s + k) % ns, "mode": m}, device_id_type=mesh)
        return 0

    lax.fori_loop(1, nm, greet_mode, 0)
    lax.fori_loop(1, ns, greet_space, 0)

    m_copy = pltpu.make_async_copy(m_hbm, m_ref, m_sem)
    m_copy.start()
    own_copy = pltpu.make_async_copy(vals_ref, cv_ref.at[m, pl.ds(0, slots)], l_sem)
    own_copy.start()

    f_bf = f_ref[...].astype(BF)
    arr_ref[A_F] = f_bf
    for side in range(2):
        hits = lax.broadcasted_iota(jnp.int32, (nodes, ghost), 0) == rows_ref[side : side + 1, :]
        picks = jnp.transpose(jnp.where(hits, 1.0, 0.0).astype(F32))
        oh_ref[side * ghost : (side + 1) * ghost, :] = picks.astype(BF)
    picked = dot(oh_ref[...], f_bf).astype(BF)
    gsend_ref[0, :, 0:width] = picked

    def zero_tail(j, _):
        cv_ref[j, slots] = jnp.zeros((width, width), BF)
        got_ref[0, j, pl.ds(3 * slab, slab), :] = jnp.zeros((slab, width), BF)
        return 0

    lax.fori_loop(0, nm, zero_tail, 0)

    @pl.when(s == 0)
    def _():
        for r in range(3):
            ghost_ref[r, 0:ghost, :] = jnp.zeros((ghost, 2 * width), BF)

    @pl.when(s == ns - 1)
    def _():
        for r in range(3):
            ghost_ref[r, ghost : 2 * ghost, :] = jnp.zeros((ghost, 2 * width), BF)

    pl.semaphore_wait(barrier, nm - 1 + ns - 1)

    wide = [width, 2 * width, width]

    def ghosts_out(r):
        w = wide[r]

        @pl.when(s > 0)
        def _():
            send(gsend_ref.at[r, pl.ds(0, ghost), pl.ds(0, w)], ghost_ref.at[r, pl.ds(ghost, ghost), pl.ds(0, w)],
                 gh_send.at[r, 0], gh_recv.at[r, 1], s - 1, m)

        @pl.when(s < ns - 1)
        def _():
            send(gsend_ref.at[r, pl.ds(ghost, ghost), pl.ds(0, w)], ghost_ref.at[r, pl.ds(0, ghost), pl.ds(0, w)],
                 gh_send.at[r, 1], gh_recv.at[r, 0], s + 1, m)

    def ghosts_in(r):
        w = wide[r]

        @pl.when(s > 0)
        def _():
            arrived(ghost_ref.at[r, pl.ds(0, ghost), pl.ds(0, w)], gh_recv.at[r, 0])

        @pl.when(s < ns - 1)
        def _():
            arrived(ghost_ref.at[r, pl.ds(ghost, ghost), pl.ds(0, w)], gh_recv.at[r, 1])

    def ghosts_sent(r):
        w = wide[r]

        @pl.when(s > 0)
        def _():
            sent(gsend_ref.at[r, pl.ds(0, ghost), pl.ds(0, w)], gh_send.at[r, 0])

        @pl.when(s < ns - 1)
        def _():
            sent(gsend_ref.at[r, pl.ds(ghost, ghost), pl.ds(0, w)], gh_send.at[r, 1])

    def spread(a):
        buf, row = PLACE[a]

        def one(k, _):
            to = (m + k) % nm
            send(arr_ref.at[a, pl.ds(to * slab, slab), :], got_ref.at[buf, m, pl.ds(row * slab, slab), :],
                 a_send.at[a, to], a_recv.at[a, m], s, to)
            return 0

        lax.fori_loop(1, nm, one, 0)
        got_ref[buf, m, pl.ds(row * slab, slab), :] = arr_ref[a, pl.ds(m * slab, slab), :]

    def first_axis(k):
        return ((y + k * c) % ny) * nx + (x + k * (1 - c)) % nx

    def moved(j, k):
        jy, jx = j // nx, j % nx
        return ((jy + k * (1 - c)) % ny) * nx + (jx + k * c) % nx

    mine = pl.ds(c * half, half)
    partner = s + 1 - 2 * c

    def table(j, h):
        return cv_ref.at[j, pl.ds(h * half, half)]

    def first_leg():
        for k in range(1, nx):
            send(vals_ref.at[mine], table(m, c), c_send.at[k - 1], c_recv.at[m, c], s, first_axis(k))
        for k in range(1, nx):
            send(vals_ref.at[mine], table(m, c), c_send.at[nx - 1 + k - 1], c_recv.at[m, c], s, moved(m, k))

    def second_leg():
        for k in range(1, nx):
            j = first_axis(nx - k)
            arrived(table(j, c), c_recv.at[j, c])
            for q in range(1, nx):
                send(table(j, c), table(j, c), c_send.at[(k + 1) * (nx - 1) + q - 1], c_recv.at[j, c], s, moved(m, q))
            send(table(j, c), table(j, c), c_send.at[nx * nx - 1 + j], c_recv.at[j, c], partner, m)

    def last_leg():
        for k in range(nx):
            for q in range(1, nx):
                j = moved(first_axis((nx - k) % nx), nx - q)
                arrived(table(j, c), c_recv.at[j, c])
                send(table(j, c), table(j, c), c_send.at[nx * nx - 1 + j], c_recv.at[j, c], partner, m)
        for k in range(1, nm):
            j = (m + k) % nm
            arrived(table(j, 1 - c), c_recv.at[j, 1 - c])

    ghosts_out(0)
    first_leg()
    spread(A_F)
    part = dot(sd_ref[...], f_bf)
    ghosts_in(0)
    sf = part + dot(sg_ref[...], ghost_ref[0, :, 0:width])
    g_high, g_low = split(force_ref[...] - sf)
    sf_bf = sf.astype(BF)
    both = jnp.concatenate([g_high, sf_bf], axis=1)
    gsend_ref[1] = dot(oh_ref[...], both).astype(BF)
    ghosts_out(1)
    arr_ref[A_SF] = sf_bf
    arr_ref[A_G] = g_high
    arr_ref[A_GLO] = g_low
    spread(A_SF)
    spread(A_G)
    spread(A_GLO)
    part = dot(sd_ref[...], both)
    ghosts_in(1)
    two = (part + dot(sg_ref[...], ghost_ref[1])).astype(BF)
    sg_bf = two[:, 0:width]
    gsend_ref[2, :, 0:width] = dot(oh_ref[...], sg_bf).astype(BF)
    ghosts_out(2)
    arr_ref[A_SG] = sg_bf
    arr_ref[A_S2F] = two[:, width : 2 * width]
    spread(A_SG)
    spread(A_S2F)
    second_leg()
    part = dot(sd_ref[...], sg_bf)
    ghosts_in(2)
    arr_ref[A_S2G] = (part + dot(sg_ref[...], ghost_ref[2, :, 0:width])).astype(BF)
    spread(A_S2G)
    last_leg()

    own_copy.wait()

    def build(t, _):
        for j in range(nm):
            c_ref[pl.ds(pl.multiple_of(t * width, width), width), j * width : (j + 1) * width] = cv_ref[j, inv_ref[t, j]]
        return 0

    lax.fori_loop(0, nm, build, 0)

    def gather(k, _):
        j = (m + k) % nm
        for a in range(7):
            buf, row = PLACE[a]
            arrived(got_ref.at[buf, j, pl.ds(row * slab, slab), :], a_recv.at[a, j])
        return 0

    lax.fori_loop(1, nm, gather, 0)

    lanes = 4 * slab

    def turn(j, _):
        rows = pl.ds(pl.multiple_of(j * width, width), width)
        xt = jnp.transpose(got_ref[0, j].astype(F32))
        x_ref[rows, 0:lanes] = (-xt).astype(BF)
        x_ref[rows, lanes : 2 * lanes] = jnp.zeros((width, lanes), BF)
        gt = jnp.transpose(got_ref[1, j].astype(F32))
        lane = lax.broadcasted_iota(jnp.int32, (width, lanes), 1)
        add_ref[rows, :] = gt + jnp.where(lane < slab, pltpu.roll(gt, slab, 1), 0.0)
        return 0

    lax.fori_loop(0, nm, turn, 0)
    m_copy.wait()

    def stage(k, _):
        prod = dot(c_ref[...], x_ref[...])
        rest = add_ref[...] + prod[:, 0:lanes] + prod[:, lanes:]
        high, low = split(rest)
        x_ref[:, 0:lanes] = high
        x_ref[:, lanes:] = low
        prod = dot(m_ref[...], x_ref[...])
        v = prod[:, 0:lanes] + prod[:, lanes:]
        v_ref[...] = v

        def back(j, _):
            rows = pl.ds(pl.multiple_of(j * width, width), width)
            block = v_ref[rows, :]
            back_src[k, j] = jnp.transpose(block)[0:slab, :]
            high, low = split(block)
            x_ref[rows, 0:lanes] = high
            x_ref[rows, lanes:] = low
            add_ref[rows, :] = pltpu.roll(block, lanes - slab, 1)
            return 0

        lax.fori_loop(0, nm, back, 0)

        def out(i, _):
            to = (m + i) % nm
            send(back_src.at[k, to], back_got.at[k, m], b_send.at[k, to], b_recv.at[k, m], s, to)
            return 0

        lax.fori_loop(1, nm, out, 0)
        back_got[k, m] = back_src[k, m]
        return 0

    lax.fori_loop(0, STEPS, stage, 0)

    def line(a, b):
        return jnp.sum(back_src[a] * back_src[b], axis=(0, 1))[None, :]

    pairs = ((0, 0), (0, 1), (1, 1), (0, 2), (1, 2), (2, 2))
    gram = jnp.concatenate([line(a, b) for a, b in pairs] + [jnp.zeros((2, width), F32)], axis=0)
    gram_src[0] = gram
    gram_got[0, m] = gram

    def reduce_mode(k, _):
        to = (m + k) % nm
        send(gram_src.at[0], gram_got.at[0, m], r_send.at[0, to], r_recv.at[0, m], s, to)
        return 0

    lax.fori_loop(1, nm, reduce_mode, 0)

    def got_mode(k, _):
        j = (m + k) % nm
        arrived(gram_got.at[0, j], r_recv.at[0, j])
        return 0

    lax.fori_loop(1, nm, got_mode, 0)
    gram = jnp.sum(gram_got[0, 0:nm], axis=0)
    gram_src[1] = gram
    gram_got[1, s] = gram

    def reduce_space(k, _):
        to = (s + k) % ns
        send(gram_src.at[1], gram_got.at[1, s], r_send.at[1, to], r_recv.at[1, s], to, m)
        return 0

    lax.fori_loop(1, ns, reduce_space, 0)

    def back_in(k, _):
        j = (m + k) % nm
        for a in range(STEPS):
            arrived(back_got.at[a, j], b_recv.at[a, j])
        return 0

    lax.fori_loop(1, nm, back_in, 0)

    def got_space(k, _):
        j = (s + k) % ns
        arrived(gram_got.at[1, j], r_recv.at[1, j])
        return 0

    lax.fori_loop(1, ns, got_space, 0)
    total = jnp.sum(jnp.sum(gram_got[1, 0:ns], axis=0), axis=1, keepdims=True) * (1.0 / (nodes * ns * nm * width))
    g00, g01, g11, g02, g12, g22 = [total[r : r + 1, :] for r in range(6)]

    def damp(mean_square):
        return step_gain / jnp.sqrt(jnp.maximum(mean_square, 0.0) + 1e-06)

    d0 = damp(g00)
    d1 = damp(g00 - 2.0 * d0 * g01 + d0 * d0 * g11)
    p, q = -(d0 + d1), d0 * d1
    d2 = damp(g00 + p * p * g11 + q * q * g22 + 2.0 * (p * g01 + q * g02 + p * q * g12))
    a0 = d0 + d1 + d2
    a1 = -d0 * d1 - d2 * (d0 + d1)
    a2 = q * d2
    for j in range(nm):
        rows = slice(j * slab, (j + 1) * slab)
        o_ref[rows, :] = f_ref[rows, :] + a0 * back_got[0, j] + a1 * back_got[1, j] + a2 * back_got[2, j]

    for r in range(3):
        ghosts_sent(r)

    def drain(k, _):
        to = (m + k) % nm
        for a in range(7):
            sent(arr_ref.at[a, pl.ds(to * slab, slab), :], a_send.at[a, to])
        for a in range(STEPS):
            sent(back_src.at[a, to], b_send.at[a, to])
        sent(gram_src.at[0], r_send.at[0, to])
        sent(table(to, c), c_send.at[nx * nx - 1 + to])
        return 0

    lax.fori_loop(1, nm, drain, 0)

    def drain_space(k, _):
        sent(gram_src.at[1], r_send.at[1, (s + k) % ns])
        return 0

    lax.fori_loop(1, ns, drain_space, 0)

    def drain_table(k, _):
        sent(vals_ref.at[mine], c_send.at[k])
        return 0

    lax.fori_loop(0, nx * nx - 1, drain_table, 0)


def solution(mesh):
    ns, nm = mesh.shape["space"], mesh.shape["mode"]
    nx = int(round(nm ** 0.5))

    def step(guess, forcing, spatial_diag, spatial_ghost, ghost_rows, chaos_vals, chaos_targets, chaos_count, mean_inverse):
        nodes, width = guess.shape
        ghost = ghost_rows.shape[1]
        blocks, slots = chaos_targets.shape
        modes = blocks * width
        slab = nodes // nm
        lanes = 4 * slab
        slot = jnp.arange(slots, dtype=jnp.int32)
        hit = chaos_targets[None, :, :] == jnp.arange(blocks, dtype=jnp.int32)[:, None, None]
        hit = hit & (slot[None, None, :] < chaos_count[None, :, None])
        inverse = slots + jnp.sum(jnp.where(hit, slot[None, None, :] - slots, 0), axis=2)
        vmem = pl.BlockSpec(memory_space=pltpu.VMEM)
        dma = pltpu.SemaphoreType.DMA
        return pl.pallas_call(
            functools.partial(kernel, (ns, nm, nx, slab, ghost, width, slots)),
            out_shape=jax.ShapeDtypeStruct((nodes, width), F32),
            in_specs=[vmem] * 6 + [pl.BlockSpec(memory_space=pltpu.SMEM), pl.BlockSpec(memory_space=pl.ANY)],
            out_specs=vmem,
            scratch_shapes=[
                pltpu.VMEM((modes, modes), BF),
                pltpu.VMEM((modes, modes), BF),
                pltpu.VMEM((nm, slots + 1, width, width), BF),
                pltpu.VMEM((2 * ghost, nodes), BF),
                pltpu.VMEM((7, nodes, width), BF),
                pltpu.VMEM((3, 2 * ghost, 2 * width), BF),
                pltpu.VMEM((3, 2 * ghost, 2 * width), BF),
                pltpu.VMEM((2, nm, lanes, width), BF),
                pltpu.VMEM((modes, 2 * lanes), BF),
                pltpu.VMEM((modes, lanes), F32),
                pltpu.VMEM((modes, lanes), F32),
                pltpu.VMEM((STEPS, nm, slab, width), F32),
                pltpu.VMEM((STEPS, nm, slab, width), F32),
                pltpu.VMEM((2, 8, width), F32),
                pltpu.VMEM((2, max(nm, ns), 8, width), F32),
                dma, dma,
                dma((3, 2)), dma((3, 2)),
                dma((7, nm)), dma((7, nm)),
                dma((nx * nx - 1 + nm,)), dma((nm, 2)),
                dma((STEPS, nm)), dma((STEPS, nm)),
                dma((2, max(nm, ns))), dma((2, max(nm, ns))),
            ],
            compiler_params=pltpu.CompilerParams(
                collective_id=0, has_side_effects=True, vmem_limit_bytes=60 * 2**20
            ),
            name="galerkin",
        )(guess, forcing, spatial_diag, spatial_ghost, ghost_rows, chaos_vals, inverse, mean_inverse)

    space, mode = P("space", "mode"), P("space", None)
    return jax.shard_map(
        step,
        mesh=mesh,
        in_specs=(space, space, mode, mode, mode, P("mode", None, None), P(), P(), P()),
        out_specs=space,
        check_vma=False,
    )
```

time: 351 us -> 97.1 us (0.28); the launches traced: 347 us -> 96.9 us
  blocking collectives: 165 us -> 0 us
  Pallas kernels: 0 us -> 93.2 us
  waiting for transfers between devices: 50.5 us -> 0 us
  matrix products: 42.9 us -> 0 us
  starting transfers between devices: 41.3 us -> 0 us
  local copies, waits for them, and re-layouts: 24 us -> 1.67 us
  between operations: 15.8 us -> 0.01 us
  other arithmetic: 7.31 us -> 2.04 us
    psum x12 -> x0, blocking collectives: 111 us -> none  [one_axis_at_a_time(): value = lax.psum(value, axis)]
    pallas_call x0 -> x1, Pallas kernels: none -> 93.2 us  [step(): pl.pallas_call(functools.partial(kernel, (ns, nm, nx, slab, ghost, width,...]
    all_to_all x5 -> x0, blocking collectives: 54.1 us -> none  [the longest x3 33.1 us: shards(): lax.all_to_all(update_slab, MODE, split_axis=1, concat_axis=0, tiled=True)]
    dot_general x10 -> x0, matrix products: 42.9 us -> none  [the longest x3 29.3 us: shards(): lax.dot_general(residual_slab, mean_inverse, (((1,), (1,)), ((), ())), pr...]
    all_gather x1 -> x0, waiting for transfers between devices: 32.4 us -> none  [shards(): slab_tables = lax.all_gather(chaos_vals, MODE, axis=0, tiled=True)]
    ppermute x6 -> x0, starting transfers between devices: 24.2 us -> none  [the longest x3 17.7 us: with_halo(): lax.ppermute(head, axis, [((i + 1) % count, i) for i in range(ends)])]
    all_to_all x4 -> x0, waiting for transfers between devices: 17.4 us -> none  [the longest x3 17.4 us: shards(): lax.all_to_all(field_bf, MODE, split_axis=0, concat_axis=1, tiled=True)]
    all_to_all x4 -> x0, starting transfers between devices: 17.2 us -> none  [the longest x3 13.6 us: shards(): lax.all_to_all(field_bf, MODE, split_axis=0, concat_axis=1, tiled=True)]
  transfers between devices with their start and end apart: 11 -> 0, of which waited for: 4 -> 0; matrix products, arithmetic and copies ran while one was open for 10% -> 0% of each run, Pallas kernels for 0% -> 0%
where the time goes in v1:
time: 97.1 us; the launch traced here: 96.9 us
  Pallas kernels  93.2 us (96%)
  other arithmetic  2.04 us (2%)
  local copies, waits for them, and re-layouts  1.67 us (2%)
    pallas_call x1, Pallas kernels, step(): pl.pallas_call(functools.partial(kernel, (ns, nm, nx, slab, ghost, width,...  93.2 us

profile of v1, /device:TPU:1, one launch (start us, length us, event | category | flops | bytes accessed | tf_op | source)
XLA Modules:
  0.0 96.9 jit_solution(6024041972053208398)
XLA Ops:
  0.0 0.7 iota_compare_fusion.1
  0.7 0.8 select_reduce_fusion
  1.4 0.6 broadcast_add_fusion.inv_ref
  2.0 93.2 %galerkin.1 = f32[512,128]{1,0:T(8,128)} custom-call(f32[512,128]{1,0:T(8,128)} %f_ref.1, f32[512,128]{1,0:T(8,128)} %force_ref.1, bf16[512,512]{1,0:T(8,128)(2,1)} %sd_ref.1, bf16[512,256]{1,0:T(8,128)(2,1)} %sg_ref.1, s32[2,128]{1,0:T(2,128)} %rows_ref.1, bf16[8,128,128]{2,1,0:T(8,128)(2,1)} %vals_ref.1, s32[16,16]{1,0:T(8,128)} %broadcast_add_fusion.inv_ref, ...), custom_call_target="tpu_custom_call" | custom-call | tf_op jit(solution)/shard_map/galerkin/pallas_call | solution.py:403
  95.2 1.7 %copy.12 = f32[512,128]{1,0:T(8,128)} copy(f32[512,128]{1,0:T(8,128)} %galerkin.1) | data formatting | bytes 524288
  (1 shorter events, 0.0 us)

commit v2 on v1

--- a/solution.py
+++ b/solution.py
@@ -26,11 +26,12 @@
 
 def kernel(
     sizes,
-    f_ref, force_ref, sd_ref, sg_ref, rows_ref, vals_ref, inv_ref, m_hbm,
+    f_hbm, force_hbm, sd_hbm, sg_hbm, rows_hbm, vals_hbm, target_ref, count_ref, m_hbm,
     o_ref,
-    m_ref, c_ref, cv_ref, oh_ref, arr_ref, gsend_ref, ghost_ref,
-    got_ref, x_ref, add_ref, v_ref, back_src, back_got, gram_src, gram_got,
-    m_sem, l_sem, gh_send, gh_recv, a_send, a_recv, c_send, c_recv, b_send, b_recv, r_send, r_recv,
+    f_ref, force_ref, sd_ref, sg_ref, rows_ref,
+    w_ref, cv_ref, slot_ref, inv_ref, oh_ref, arr_ref, gsend_ref, ghost_ref,
+    got_ref, x_ref, add_ref, back_src, back_got, gram_src, gram_got,
+    l_sem, gh_send, gh_recv, a_send, a_recv, c_send, c_recv, b_send, b_recv, r_send, r_recv,
 ):
     ns, nm, nx, slab, ghost, width, slots = sizes
     ny = nm // nx
@@ -73,10 +74,17 @@
     lax.fori_loop(1, nm, greet_mode, 0)
     lax.fori_loop(1, ns, greet_space, 0)
 
-    m_copy = pltpu.make_async_copy(m_hbm, m_ref, m_sem)
-    m_copy.start()
-    own_copy = pltpu.make_async_copy(vals_ref, cv_ref.at[m, pl.ds(0, slots)], l_sem)
-    own_copy.start()
+    loads = [
+        pltpu.make_async_copy(src, dst, l_sem.at[n])
+        for n, (src, dst) in enumerate((
+            (f_hbm, f_ref), (rows_hbm, rows_ref), (vals_hbm, cv_ref.at[m, pl.ds(0, slots)]),
+            (sd_hbm, sd_ref), (sg_hbm, sg_ref), (force_hbm, force_ref), (m_hbm, w_ref.at[1]),
+        ))
+    ]
+    for load in loads:
+        load.start()
+    loads[0].wait()
+    loads[1].wait()
 
     f_bf = f_ref[...].astype(BF)
     arr_ref[A_F] = f_bf
@@ -90,6 +98,7 @@
     def zero_tail(j, _):
         cv_ref[j, slots] = jnp.zeros((width, width), BF)
         got_ref[0, j, pl.ds(3 * slab, slab), :] = jnp.zeros((slab, width), BF)
+        add_ref[1, pl.ds(pl.multiple_of(j * width, width), width), :] = jnp.zeros((width, 4 * slab), F32)
         return 0
 
     lax.fori_loop(0, nm, zero_tail, 0)
@@ -155,47 +164,79 @@
         lax.fori_loop(1, nm, one, 0)
         got_ref[buf, m, pl.ds(row * slab, slab), :] = arr_ref[a, pl.ds(m * slab, slab), :]
 
-    def first_axis(k):
-        return ((y + k * c) % ny) * nx + (x + k * (1 - c)) % nx
-
-    def moved(j, k):
-        jy, jx = j // nx, j % nx
-        return ((jy + k * (1 - c)) % ny) * nx + (jx + k * c) % nx
-
-    mine = pl.ds(c * half, half)
+    def along(a, b):
+        return ((y + a * c + b * (1 - c) + 2 * nx) % ny) * nx + (x + a * (1 - c) + b * c + 2 * nx) % nx
+
     partner = s + 1 - 2 * c
+    leaving = []
 
     def table(j, h):
         return cv_ref.at[j, pl.ds(h * half, half)]
 
-    def first_leg():
-        for k in range(1, nx):
-            send(vals_ref.at[mine], table(m, c), c_send.at[k - 1], c_recv.at[m, c], s, first_axis(k))
-        for k in range(1, nx):
-            send(vals_ref.at[mine], table(m, c), c_send.at[nx - 1 + k - 1], c_recv.at[m, c], s, moved(m, k))
-
-    def second_leg():
-        for k in range(1, nx):
-            j = first_axis(nx - k)
-            arrived(table(j, c), c_recv.at[j, c])
-            for q in range(1, nx):
-                send(table(j, c), table(j, c), c_send.at[(k + 1) * (nx - 1) + q - 1], c_recv.at[j, c], s, moved(m, q))
-            send(table(j, c), table(j, c), c_send.at[nx * nx - 1 + j], c_recv.at[j, c], partner, m)
-
-    def last_leg():
-        for k in range(nx):
-            for q in range(1, nx):
-                j = moved(first_axis((nx - k) % nx), nx - q)
-                arrived(table(j, c), c_recv.at[j, c])
-                send(table(j, c), table(j, c), c_send.at[nx * nx - 1 + j], c_recv.at[j, c], partner, m)
-        for k in range(1, nm):
+    def part_of(j, q):
+        return cv_ref.at[j, pl.ds(c * half + q * (half // 2), half // 2)]
+
+    def post(ref, j, to_s, to_m):
+        sem = c_send.at[len(leaving)]
+        leaving.append((ref, sem))
+        send(ref, ref, sem, c_recv.at[j, c], to_s, to_m)
+
+    def await_table(a, b):
+        j = along(a, b)
+        arrived(table(j, c), c_recv.at[j, c])
+        post(table(j, c), j, partner, m)
+        return j
+
+    def fan_first():
+        post(table(m, c), m, s, along(1, 0))
+        post(table(m, c), m, s, along(-1, 0))
+        post(table(m, c), m, s, along(0, 1))
+        post(table(m, c), m, s, along(0, -1))
+
+    def pass_first(a):
+        j = await_table(a, 0)
+        post(part_of(j, 0 if a < 0 else 1), j, s, along(-a, 0))
+        post(table(j, c), j, s, along(0, 1))
+        post(table(j, c), j, s, along(0, -1))
+
+    def pass_second(a):
+        for b in (-1, 1):
+            j = await_table(a, b)
+            post(part_of(j, 0 if b < 0 else 1), j, s, along(0, -b))
+
+    def tables_one():
+        pass_first(-1)
+        pass_first(1)
+        pass_second(0)
+
+    def tables_two():
+        j = await_table(2, 0)
+        post(table(j, c), j, s, along(0, 1))
+        post(table(j, c), j, s, along(0, -1))
+        pass_second(-1)
+        pass_second(1)
+
+    def tables_three():
+        pass_second(2)
+        for a in (0, -1, 1, 2):
+            await_table(a, 2)
+
+    def tables_other():
+        def one(k, _):
             j = (m + k) % nm
             arrived(table(j, 1 - c), c_recv.at[j, 1 - c])
+            return 0
+
+        lax.fori_loop(1, nm, one, 0)
 
     ghosts_out(0)
-    first_leg()
+    loads[2].wait()
+    fan_first()
     spread(A_F)
+    loads[3].wait()
     part = dot(sd_ref[...], f_bf)
+    loads[4].wait()
+    loads[5].wait()
     ghosts_in(0)
     sf = part + dot(sg_ref[...], ghost_ref[0, :, 0:width])
     g_high, g_low = split(force_ref[...] - sf)
@@ -206,6 +247,7 @@
     arr_ref[A_SF] = sf_bf
     arr_ref[A_G] = g_high
     arr_ref[A_GLO] = g_low
+    tables_one()
     spread(A_SF)
     spread(A_G)
     spread(A_GLO)
@@ -219,68 +261,93 @@
     arr_ref[A_S2F] = two[:, width : 2 * width]
     spread(A_SG)
     spread(A_S2F)
-    second_leg()
+    tables_two()
     part = dot(sd_ref[...], sg_bf)
     ghosts_in(2)
     arr_ref[A_S2G] = (part + dot(sg_ref[...], ghost_ref[2, :, 0:width])).astype(BF)
     spread(A_S2G)
-    last_leg()
-
-    own_copy.wait()
+    tables_three()
+
+    blocks = target_ref.shape[0]
+    lane = lax.broadcasted_iota(jnp.int32, (blocks, 128), 1)
+    line_no = lax.broadcasted_iota(jnp.int32, (blocks, 128), 0)
+    used = jnp.zeros((blocks, 128), jnp.int32)
+    for j in range(blocks):
+        used = jnp.where(line_no == j, count_ref[j], used)
+    found = jnp.full((blocks, 128), slots, jnp.int32)
+    for q in range(slots):
+        found = jnp.where((target_ref[:, q : q + 1] == lane) & (used > q), q, found)
+    slot_ref[...] = found
+    table_copy = pltpu.make_async_copy(slot_ref, inv_ref, l_sem.at[7])
+    table_copy.start()
+
+    lanes = 4 * slab
+
+    def gather(buf):
+        def one(k, _):
+            j = (m + k) % nm
+            for a in range(7):
+                if PLACE[a][0] == buf:
+                    arrived(got_ref.at[buf, j, pl.ds(PLACE[a][1] * slab, slab), :], a_recv.at[a, j])
+            return 0
+
+        lax.fori_loop(1, nm, one, 0)
+
+    def turn_x(j, _):
+        rows = pl.ds(pl.multiple_of(j * width, width), width)
+        x_ref[0, rows, 0:lanes] = (-jnp.transpose(got_ref[0, j].astype(F32))).astype(BF)
+        x_ref[0, rows, lanes : 2 * lanes] = jnp.zeros((width, lanes), BF)
+        return 0
+
+    def turn_g(j, _):
+        rows = pl.ds(pl.multiple_of(j * width, width), width)
+        gt = jnp.transpose(got_ref[1, j].astype(F32))
+        at = lax.broadcasted_iota(jnp.int32, (width, lanes), 1)
+        add_ref[0, rows, :] = gt + jnp.where(at < slab, pltpu.roll(gt, slab, 1), 0.0)
+        return 0
+
+    gather(0)
+    lax.fori_loop(0, nm, turn_x, 0)
+    gather(1)
+    lax.fori_loop(0, nm, turn_g, 0)
+    tables_other()
+    table_copy.wait()
 
     def build(t, _):
         for j in range(nm):
-            c_ref[pl.ds(pl.multiple_of(t * width, width), width), j * width : (j + 1) * width] = cv_ref[j, inv_ref[t, j]]
+            w_ref[0, pl.ds(pl.multiple_of(t * width, width), width), j * width : (j + 1) * width] = cv_ref[j, inv_ref[j, t]]
         return 0
 
     lax.fori_loop(0, nm, build, 0)
-
-    def gather(k, _):
-        j = (m + k) % nm
-        for a in range(7):
-            buf, row = PLACE[a]
-            arrived(got_ref.at[buf, j, pl.ds(row * slab, slab), :], a_recv.at[a, j])
-        return 0
-
-    lax.fori_loop(1, nm, gather, 0)
-
-    lanes = 4 * slab
-
-    def turn(j, _):
-        rows = pl.ds(pl.multiple_of(j * width, width), width)
-        xt = jnp.transpose(got_ref[0, j].astype(F32))
-        x_ref[rows, 0:lanes] = (-xt).astype(BF)
-        x_ref[rows, lanes : 2 * lanes] = jnp.zeros((width, lanes), BF)
-        gt = jnp.transpose(got_ref[1, j].astype(F32))
-        lane = lax.broadcasted_iota(jnp.int32, (width, lanes), 1)
-        add_ref[rows, :] = gt + jnp.where(lane < slab, pltpu.roll(gt, slab, 1), 0.0)
-        return 0
-
-    lax.fori_loop(0, nm, turn, 0)
-    m_copy.wait()
-
-    def stage(k, _):
-        prod = dot(c_ref[...], x_ref[...])
-        rest = add_ref[...] + prod[:, 0:lanes] + prod[:, lanes:]
-        high, low = split(rest)
-        x_ref[:, 0:lanes] = high
-        x_ref[:, lanes:] = low
-        prod = dot(m_ref[...], x_ref[...])
-        v = prod[:, 0:lanes] + prod[:, lanes:]
-        v_ref[...] = v
-
-        def back(j, _):
-            rows = pl.ds(pl.multiple_of(j * width, width), width)
-            block = v_ref[rows, :]
-            back_src[k, j] = jnp.transpose(block)[0:slab, :]
-            high, low = split(block)
-            x_ref[rows, 0:lanes] = high
-            x_ref[rows, lanes:] = low
-            add_ref[rows, :] = pltpu.roll(block, lanes - slab, 1)
+    loads[6].wait()
+
+    rows_at_once = nm * width // 2
+
+    def apply(p, _):
+        odd = p % 2
+
+        def some(q, _):
+            base = pl.multiple_of(q * rows_at_once, rows_at_once)
+            rows = pl.ds(base, rows_at_once)
+            prod = dot(w_ref[odd, rows, :], x_ref[odd])
+            value = add_ref[odd, rows, :] + prod[:, 0:lanes] + prod[:, lanes:]
+            high, low = split(value)
+            x_ref[1 - odd, rows, 0:lanes] = high
+            x_ref[1 - odd, rows, lanes:] = low
+            add_ref[2 - 2 * odd, rows, :] = pltpu.roll(value, lanes - slab, 1)
+            for r in range(nm // 2):
+                back_src[p // 2, q * (nm // 2) + r] = jnp.transpose(value[r * width : (r + 1) * width, :])[0:slab, :]
             return 0
 
-        lax.fori_loop(0, nm, back, 0)
-
+        lax.fori_loop(0, 2, some, 0)
+
+        @pl.when((p == 1) | (p == 3))
+        def _():
+            back_out(p // 2)
+
+        return 0
+
+    def back_out(k):
         def out(i, _):
             to = (m + i) % nm
             send(back_src.at[k, to], back_got.at[k, m], b_send.at[k, to], b_recv.at[k, m], s, to)
@@ -288,9 +355,8 @@
 
         lax.fori_loop(1, nm, out, 0)
         back_got[k, m] = back_src[k, m]
-        return 0
-
-    lax.fori_loop(0, STEPS, stage, 0)
+
+    lax.fori_loop(0, 2 * STEPS, apply, 0)
 
     def line(a, b):
         return jnp.sum(back_src[a] * back_src[b], axis=(0, 1))[None, :]
@@ -306,6 +372,7 @@
         return 0
 
     lax.fori_loop(1, nm, reduce_mode, 0)
+    back_out(STEPS - 1)
 
     def got_mode(k, _):
         j = (m + k) % nm
@@ -351,9 +418,7 @@
     a0 = d0 + d1 + d2
     a1 = -d0 * d1 - d2 * (d0 + d1)
     a2 = q * d2
-    for j in range(nm):
-        rows = slice(j * slab, (j + 1) * slab)
-        o_ref[rows, :] = f_ref[rows, :] + a0 * back_got[0, j] + a1 * back_got[1, j] + a2 * back_got[2, j]
+    o_ref[...] = a0 * back_got[0] + a1 * back_got[1] + a2 * back_got[2]
 
     for r in range(3):
         ghosts_sent(r)
@@ -365,7 +430,6 @@
         for a in range(STEPS):
             sent(back_src.at[a, to], b_send.at[a, to])
         sent(gram_src.at[0], r_send.at[0, to])
-        sent(table(to, c), c_send.at[nx * nx - 1 + to])
         return 0
 
     lax.fori_loop(1, nm, drain, 0)
@@ -376,11 +440,8 @@
 
     lax.fori_loop(1, ns, drain_space, 0)
 
-    def drain_table(k, _):
-        sent(vals_ref.at[mine], c_send.at[k])
-        return 0
-
-    lax.fori_loop(0, nx * nx - 1, drain_table, 0)
+    for ref, sem in leaving:
+        sent(ref, sem)
 
 
 def solution(mesh):
@@ -394,37 +455,39 @@
         modes = blocks * width
         slab = nodes // nm
         lanes = 4 * slab
-        slot = jnp.arange(slots, dtype=jnp.int32)
-        hit = chaos_targets[None, :, :] == jnp.arange(blocks, dtype=jnp.int32)[:, None, None]
-        hit = hit & (slot[None, None, :] < chaos_count[None, :, None])
-        inverse = slots + jnp.sum(jnp.where(hit, slot[None, None, :] - slots, 0), axis=2)
         vmem = pl.BlockSpec(memory_space=pltpu.VMEM)
         dma = pltpu.SemaphoreType.DMA
-        return pl.pallas_call(
+        smem, anywhere = pl.BlockSpec(memory_space=pltpu.SMEM), pl.BlockSpec(memory_space=pl.ANY)
+        gathered = pl.pallas_call(
             functools.partial(kernel, (ns, nm, nx, slab, ghost, width, slots)),
-            out_shape=jax.ShapeDtypeStruct((nodes, width), F32),
-            in_specs=[vmem] * 6 + [pl.BlockSpec(memory_space=pltpu.SMEM), pl.BlockSpec(memory_space=pl.ANY)],
+            out_shape=jax.ShapeDtypeStruct((nm, slab, width), F32),
+            in_specs=[anywhere] * 6 + [vmem, smem, anywhere],
             out_specs=vmem,
             scratch_shapes=[
-                pltpu.VMEM((modes, modes), BF),
-                pltpu.VMEM((modes, modes), BF),
+                pltpu.VMEM((nodes, width), F32),
+                pltpu.VMEM((nodes, width), F32),
+                pltpu.VMEM((nodes, nodes), BF),
+                pltpu.VMEM((nodes, 2 * ghost), BF),
+                pltpu.VMEM((2, ghost), jnp.int32),
+                pltpu.VMEM((2, modes, modes), BF),
                 pltpu.VMEM((nm, slots + 1, width, width), BF),
+                pltpu.VMEM((blocks, 128), jnp.int32),
+                pltpu.SMEM((blocks, 128), jnp.int32),
                 pltpu.VMEM((2 * ghost, nodes), BF),
                 pltpu.VMEM((7, nodes, width), BF),
                 pltpu.VMEM((3, 2 * ghost, 2 * width), BF),
                 pltpu.VMEM((3, 2 * ghost, 2 * width), BF),
                 pltpu.VMEM((2, nm, lanes, width), BF),
-                pltpu.VMEM((modes, 2 * lanes), BF),
-                pltpu.VMEM((modes, lanes), F32),
-                pltpu.VMEM((modes, lanes), F32),
+                pltpu.VMEM((2, modes, 2 * lanes), BF),
+                pltpu.VMEM((3, modes, lanes), F32),
                 pltpu.VMEM((STEPS, nm, slab, width), F32),
                 pltpu.VMEM((STEPS, nm, slab, width), F32),
                 pltpu.VMEM((2, 8, width), F32),
                 pltpu.VMEM((2, max(nm, ns), 8, width), F32),
-                dma, dma,
+                dma((8,)),
                 dma((3, 2)), dma((3, 2)),
                 dma((7, nm)), dma((7, nm)),
-                dma((nx * nx - 1 + nm,)), dma((nm, 2)),
+                dma((40,)), dma((nm, 2)),
                 dma((STEPS, nm)), dma((STEPS, nm)),
                 dma((2, max(nm, ns))), dma((2, max(nm, ns))),
             ],
@@ -432,7 +495,8 @@
                 collective_id=0, has_side_effects=True, vmem_limit_bytes=60 * 2**20
             ),
             name="galerkin",
-        )(guess, forcing, spatial_diag, spatial_ghost, ghost_rows, chaos_vals, inverse, mean_inverse)
+        )(guess, forcing, spatial_diag, spatial_ghost, ghost_rows, chaos_vals, chaos_targets, chaos_count, mean_inverse)
+        return guess + gathered.reshape(nodes, width)
 
     space, mode = P("space", "mode"), P("space", None)
     return jax.shard_map(

time: 97.1 us -> 80.8 us (0.83)
  Pallas kernels: 93.2 us -> 77.5 us
    pallas_call x1, Pallas kernels: 93.2 us -> 77.5 us  [step(): pl.pallas_call(functools.partial(kernel, (ns, nm, nx, slab, ghost, width,...]
    add x1, other arithmetic: 0.6 us -> 1.68 us  [step(): return guess + gathered.reshape(nodes, width)]
where the time goes in v2:
time: 80.8 us; the launch traced here: 80.6 us
  Pallas kernels  77.5 us (96%)
  other arithmetic  1.68 us (2%)
  local copies, waits for them, and re-layouts  1.4 us (2%)
    pallas_call x1, Pallas kernels, step(): pl.pallas_call(functools.partial(kernel, (ns, nm, nx, slab, ghost, width,...  77.5 us
    add x1, other arithmetic, step(): return guess + gathered.reshape(nodes, width)  1.68 us

profile of v2, /device:TPU:1, one launch (start us, length us, event | category | flops | bytes accessed | tf_op | source)
XLA Modules:
  0.0 80.6 jit_solution(12032221403557204775)
XLA Ops:
  0.0 0.0 copy-start
  0.0 1.4 %copy.10.target_ref = s32[16,8]{1,0:T(8,128)} copy(s32[16,8]{0,1:T(8,128)} %param.15) | data formatting | bytes 1024 | tf_op args[6]
  1.4 77.5 %galerkin.1 = f32[16,32,128]{2,1,0:T(8,128)} custom-call(f32[512,128]{1,0:T(8,128)} %f_hbm.1, f32[512,128]{1,0:T(8,128)} %force_hbm.1, bf16[512,512]{1,0:T(8,128)(2,1)} %sd_hbm.1, bf16[512,256]{1,0:T(8,128)(2,1)} %sg_hbm.1, s32[2,128]{1,0:T(2,128)} %rows_hbm.1, bf16[8,128,128]{2,1,0:T(8,128)(2,1)} %vals_hbm.1, s32[16,8]{1,0:T(8,128)} %copy.10.target_ref, ...), custom_call_target="tpu_custom_call" | custom-call | tf_op jit(solution)/shard_map/galerkin/pallas_call | solution.py:461
  79.0 0.0 copy-done
  79.0 1.7 %bitcast_add_fusion = f32[512,128]{1,0:T(8,128)} fusion(f32[512,128]{1,0:T(8,128)S(1)} %copy-done, f32[16,32,128]{2,1,0:T(8,128)} %galerkin.1), kind=kLoop, calls=%fused_computation | loop fusion | flops 65536 | bytes 786432 | tf_op jit(solution)/shard_map/add | solution.py:499
Async XLA Ops:
  0.0 79.0 %copy-start = (f32[512,128]{1,0:T(8,128)S(1)}, f32[512,128]{1,0:T(8,128)}, u32[]{:S(2)}) copy-start(f32[512,128]{1,0:T(8,128)} %f_hbm.1) | copy-start | bytes 786436

commit v3 on v2

--- a/solution.py
+++ b/solution.py
@@ -30,12 +30,11 @@
     o_ref,
     f_ref, force_ref, sd_ref, sg_ref, rows_ref,
     w_ref, cv_ref, slot_ref, inv_ref, oh_ref, arr_ref, gsend_ref, ghost_ref,
-    got_ref, x_ref, add_ref, back_src, back_got, gram_src, gram_got,
-    l_sem, gh_send, gh_recv, a_send, a_recv, c_send, c_recv, b_send, b_recv, r_send, r_recv,
+    got_ref, x_ref, add_ref, back_src, back_got, last_src, last_got, gram_src, gram_got,
+    l_sem, gh_send, gh_recv, a_send, a_recv, c_send, z_send, c_recv, b_send, b_recv, r_send, r_recv,
 ):
     ns, nm, nx, slab, ghost, width, slots = sizes
     ny = nm // nx
-    half = slots // 2
     nodes = f_ref.shape[0]
     s, m = lax.axis_index("space"), lax.axis_index("mode")
     c = s % 2
@@ -113,6 +112,8 @@
         for r in range(3):
             ghost_ref[r, ghost : 2 * ghost, :] = jnp.zeros((ghost, 2 * width), BF)
 
+    loads[3].wait()
+    part = dot(sd_ref[...], f_bf)
     pl.semaphore_wait(barrier, nm - 1 + ns - 1)
 
     wide = [width, 2 * width, width]
@@ -164,45 +165,53 @@
         lax.fori_loop(1, nm, one, 0)
         got_ref[buf, m, pl.ds(row * slab, slab), :] = arr_ref[a, pl.ds(m * slab, slab), :]
 
+    pair = slots // 4
+    level = (s // 2) % 2
+    base, far = level * 2 * pair + c * pair, (1 - level) * 2 * pair + c * pair
+    partner, above, below = s + 1 - 2 * c, (s + 2) % ns, (s + ns - 2) % ns
+    leaving = []
+
     def along(a, b):
         return ((y + a * c + b * (1 - c) + 2 * nx) % ny) * nx + (x + a * (1 - c) + b * c + 2 * nx) % nx
 
-    partner = s + 1 - 2 * c
-    leaving = []
-
-    def table(j, h):
-        return cv_ref.at[j, pl.ds(h * half, half)]
-
-    def part_of(j, q):
-        return cv_ref.at[j, pl.ds(c * half + q * (half // 2), half // 2)]
-
-    def post(ref, j, to_s, to_m):
+    def table(j, first, count=pair):
+        return cv_ref.at[j, pl.ds(first, count)]
+
+    def post(ref, j, kind, to_s, to_m):
         sem = c_send.at[len(leaving)]
         leaving.append((ref, sem))
-        send(ref, ref, sem, c_recv.at[j, c], to_s, to_m)
+        send(ref, ref, sem, c_recv.at[j, kind], to_s, to_m)
 
     def await_table(a, b):
         j = along(a, b)
-        arrived(table(j, c), c_recv.at[j, c])
-        post(table(j, c), j, partner, m)
+        arrived(table(j, base), c_recv.at[j, 0])
         return j
 
+    def share(j):
+        post(table(j, base, pair // 2), j, 1, above, m)
+        post(table(j, base + pair // 2, pair // 2), j, 1, below, m)
+        post(table(j, base), j, 2, partner, m)
+
+    def both_ways(j):
+        post(table(j, base), j, 0, s, along(0, 1))
+        post(table(j, base), j, 0, s, along(0, -1))
+
     def fan_first():
-        post(table(m, c), m, s, along(1, 0))
-        post(table(m, c), m, s, along(-1, 0))
-        post(table(m, c), m, s, along(0, 1))
-        post(table(m, c), m, s, along(0, -1))
+        post(table(m, base), m, 0, s, along(1, 0))
+        post(table(m, base), m, 0, s, along(-1, 0))
+        both_ways(m)
 
     def pass_first(a):
         j = await_table(a, 0)
-        post(part_of(j, 0 if a < 0 else 1), j, s, along(-a, 0))
-        post(table(j, c), j, s, along(0, 1))
-        post(table(j, c), j, s, along(0, -1))
+        post(table(j, base + (0 if a < 0 else pair // 2), pair // 2), j, 0, s, along(-a, 0))
+        both_ways(j)
+        share(j)
 
     def pass_second(a):
         for b in (-1, 1):
             j = await_table(a, b)
-            post(part_of(j, 0 if b < 0 else 1), j, s, along(0, -b))
+            post(table(j, base + (0 if b < 0 else pair // 2), pair // 2), j, 0, s, along(0, -b))
+            share(j)
 
     def tables_one():
         pass_first(-1)
@@ -211,30 +220,37 @@
 
     def tables_two():
         j = await_table(2, 0)
-        post(table(j, c), j, s, along(0, 1))
-        post(table(j, c), j, s, along(0, -1))
+        both_ways(j)
+        share(j)
         pass_second(-1)
         pass_second(1)
 
     def tables_three():
         pass_second(2)
         for a in (0, -1, 1, 2):
-            await_table(a, 2)
+            share(await_table(a, 2))
 
     def tables_other():
-        def one(k, _):
+        def level_in(k, _):
             j = (m + k) % nm
-            arrived(table(j, 1 - c), c_recv.at[j, 1 - c])
+            arrived(table(j, far), c_recv.at[j, 1])
+            send(table(j, far), table(j, far), z_send.at[j], c_recv.at[j, 3], partner, m)
             return 0
 
-        lax.fori_loop(1, nm, one, 0)
+        lax.fori_loop(1, nm, level_in, 0)
+
+        def core_in(k, _):
+            j = (m + k) % nm
+            arrived(table(j, base + pair - 2 * c * pair), c_recv.at[j, 2])
+            arrived(table(j, far + pair - 2 * c * pair), c_recv.at[j, 3])
+            return 0
+
+        lax.fori_loop(1, nm, core_in, 0)
 
     ghosts_out(0)
     loads[2].wait()
     fan_first()
     spread(A_F)
-    loads[3].wait()
-    part = dot(sd_ref[...], f_bf)
     loads[4].wait()
     loads[5].wait()
     ghosts_in(0)
@@ -268,16 +284,17 @@
     spread(A_S2G)
     tables_three()
 
-    blocks = target_ref.shape[0]
-    lane = lax.broadcasted_iota(jnp.int32, (blocks, 128), 1)
-    line_no = lax.broadcasted_iota(jnp.int32, (blocks, 128), 0)
-    used = jnp.zeros((blocks, 128), jnp.int32)
+    blocks = target_ref.shape[1]
+    lane = lax.broadcasted_iota(jnp.int32, (blocks, blocks), 1)
+    goal = lax.broadcasted_iota(jnp.int32, (blocks, blocks), 0)
+    used = jnp.zeros((blocks, blocks), jnp.int32)
     for j in range(blocks):
-        used = jnp.where(line_no == j, count_ref[j], used)
-    found = jnp.full((blocks, 128), slots, jnp.int32)
+        used = jnp.where(lane == j, count_ref[j], used)
+    found = jnp.full((blocks, blocks), slots, jnp.int32)
     for q in range(slots):
-        found = jnp.where((target_ref[:, q : q + 1] == lane) & (used > q), q, found)
-    slot_ref[...] = found
+        found = jnp.where((target_ref[q : q + 1, :] == goal) & (used > q), q, found)
+    slot_ref[...] = jnp.zeros((blocks, 128), jnp.int32)
+    slot_ref[:, 0:blocks] = found
     table_copy = pltpu.make_async_copy(slot_ref, inv_ref, l_sem.at[7])
     table_copy.start()
 
@@ -315,7 +332,7 @@
 
     def build(t, _):
         for j in range(nm):
-            w_ref[0, pl.ds(pl.multiple_of(t * width, width), width), j * width : (j + 1) * width] = cv_ref[j, inv_ref[j, t]]
+            w_ref[0, pl.ds(pl.multiple_of(t * width, width), width), j * width : (j + 1) * width] = cv_ref[j, inv_ref[t, j]]
         return 0
 
     lax.fori_loop(0, nm, build, 0)
@@ -335,26 +352,38 @@
             x_ref[1 - odd, rows, 0:lanes] = high
             x_ref[1 - odd, rows, lanes:] = low
             add_ref[2 - 2 * odd, rows, :] = pltpu.roll(value, lanes - slab, 1)
-            for r in range(nm // 2):
-                back_src[p // 2, q * (nm // 2) + r] = jnp.transpose(value[r * width : (r + 1) * width, :])[0:slab, :]
             return 0
 
         lax.fori_loop(0, 2, some, 0)
 
+        @pl.when(odd == 1)
+        def _():
+            def turn_back(j, _):
+                block = add_ref[0, pl.ds(pl.multiple_of(j * width, width), width), :]
+                back_src[p // 2, j] = jnp.transpose(block)[lanes - slab :, :]
+                return 0
+
+            lax.fori_loop(0, nm, turn_back, 0, unroll=2)
+
         @pl.when((p == 1) | (p == 3))
         def _():
             back_out(p // 2)
 
         return 0
 
+    def back_dst(a, many, one):
+        return one if isinstance(a, int) and a == STEPS - 1 else many.at[a]
+
     def back_out(k):
+        src, dst = back_dst(k, back_src, last_src), back_dst(k, back_got, last_got)
+
         def out(i, _):
             to = (m + i) % nm
-            send(back_src.at[k, to], back_got.at[k, m], b_send.at[k, to], b_recv.at[k, m], s, to)
+            send(src.at[to], dst.at[m], b_send.at[k, to], b_recv.at[k, m], s, to)
             return 0
 
         lax.fori_loop(1, nm, out, 0)
-        back_got[k, m] = back_src[k, m]
+        dst[m] = src[m]
 
     lax.fori_loop(0, 2 * STEPS, apply, 0)
 
@@ -372,6 +401,7 @@
         return 0
 
     lax.fori_loop(1, nm, reduce_mode, 0)
+    last_src[...] = back_src[STEPS - 1].astype(BF)
     back_out(STEPS - 1)
 
     def got_mode(k, _):
@@ -394,7 +424,7 @@
     def back_in(k, _):
         j = (m + k) % nm
         for a in range(STEPS):
-            arrived(back_got.at[a, j], b_recv.at[a, j])
+            arrived(back_dst(a, back_got, last_got).at[j], b_recv.at[a, j])
         return 0
 
     lax.fori_loop(1, nm, back_in, 0)
@@ -418,7 +448,7 @@
     a0 = d0 + d1 + d2
     a1 = -d0 * d1 - d2 * (d0 + d1)
     a2 = q * d2
-    o_ref[...] = a0 * back_got[0] + a1 * back_got[1] + a2 * back_got[2]
+    o_ref[...] = a0 * back_got[0] + a1 * back_got[1] + a2 * last_got[...].astype(F32)
 
     for r in range(3):
         ghosts_sent(r)
@@ -428,8 +458,9 @@
         for a in range(7):
             sent(arr_ref.at[a, pl.ds(to * slab, slab), :], a_send.at[a, to])
         for a in range(STEPS):
-            sent(back_src.at[a, to], b_send.at[a, to])
+            sent(back_dst(a, back_src, last_src).at[to], b_send.at[a, to])
         sent(gram_src.at[0], r_send.at[0, to])
+        sent(table(to, far), z_send.at[to])
         return 0
 
     lax.fori_loop(1, nm, drain, 0)
@@ -481,13 +512,15 @@
                 pltpu.VMEM((2, modes, 2 * lanes), BF),
                 pltpu.VMEM((3, modes, lanes), F32),
                 pltpu.VMEM((STEPS, nm, slab, width), F32),
-                pltpu.VMEM((STEPS, nm, slab, width), F32),
+                pltpu.VMEM((STEPS - 1, nm, slab, width), F32),
+                pltpu.VMEM((nm, slab, width), BF),
+                pltpu.VMEM((nm, slab, width), BF),
                 pltpu.VMEM((2, 8, width), F32),
                 pltpu.VMEM((2, max(nm, ns), 8, width), F32),
                 dma((8,)),
                 dma((3, 2)), dma((3, 2)),
                 dma((7, nm)), dma((7, nm)),
-                dma((40,)), dma((nm, 2)),
+                dma((72,)), dma((nm,)), dma((nm, 4)),
                 dma((STEPS, nm)), dma((STEPS, nm)),
                 dma((2, max(nm, ns))), dma((2, max(nm, ns))),
             ],
@@ -495,7 +528,7 @@
                 collective_id=0, has_side_effects=True, vmem_limit_bytes=60 * 2**20
             ),
             name="galerkin",
-        )(guess, forcing, spatial_diag, spatial_ghost, ghost_rows, chaos_vals, chaos_targets, chaos_count, mean_inverse)
+        )(guess, forcing, spatial_diag, spatial_ghost, ghost_rows, chaos_vals, chaos_targets.T, chaos_count, mean_inverse)
         return guess + gathered.reshape(nodes, width)
 
     space, mode = P("space", "mode"), P("space", None)

time: 80.8 us -> 77.8 us (0.963)
  Pallas kernels: 77.5 us -> 76 us
  local copies, waits for them, and re-layouts: 1.4 us -> 0.01 us
    pallas_call x1, Pallas kernels: 77.5 us -> 76 us  [step(): pl.pallas_call(functools.partial(kernel, (ns, nm, nx, slab, ghost, width,...]
    unnamed x3 -> x2, local copies, waits for them, and re-layouts: 1.4 us -> 0.01 us
where the time goes in v3:
time: 77.8 us; the launch traced here: 77.7 us
  Pallas kernels  76 us (98%)
  other arithmetic  1.68 us (2%)
    pallas_call x1, Pallas kernels, step(): pl.pallas_call(functools.partial(kernel, (ns, nm, nx, slab, ghost, width,...  76 us
    add x1, other arithmetic, step(): return guess + gathered.reshape(nodes, width)  1.68 us

profile of v3, /device:TPU:1, one launch (start us, length us, event | category | flops | bytes accessed | tf_op | source)
XLA Modules:
  0.0 77.7 jit_solution(8999328487304392829)
XLA Ops:
  0.0 0.0 copy-start
  0.0 76.0 %galerkin.1 = f32[16,32,128]{2,1,0:T(8,128)} custom-call(f32[512,128]{1,0:T(8,128)} %f_hbm.1, f32[512,128]{1,0:T(8,128)} %force_hbm.1, bf16[512,512]{1,0:T(8,128)(2,1)} %sd_hbm.1, bf16[512,256]{1,0:T(8,128)(2,1)} %sg_hbm.1, s32[2,128]{1,0:T(2,128)} %rows_hbm.1, bf16[8,128,128]{2,1,0:T(8,128)(2,1)} %vals_hbm.1, s32[8,16]{1,0:T(8,128)} %bitcast.3, ...), custom_call_target="tpu_custom_call" | custom-call | tf_op jit(solution)/shard_map/galerkin/pallas_call | solution.py:492
  76.0 0.0 copy-done
  76.0 1.7 %bitcast_add_fusion = f32[512,128]{1,0:T(8,128)} fusion(f32[512,128]{1,0:T(8,128)S(1)} %copy-done, f32[16,32,128]{2,1,0:T(8,128)} %galerkin.1), kind=kLoop, calls=%fused_computation | loop fusion | flops 65536 | bytes 786432 | tf_op jit(solution)/shard_map/add | solution.py:532
Async XLA Ops:
  0.0 76.0 %copy-start = (f32[512,128]{1,0:T(8,128)S(1)}, f32[512,128]{1,0:T(8,128)}, u32[]{:S(2)}) copy-start(f32[512,128]{1,0:T(8,128)} %f_hbm.1) | copy-start | bytes 786436

commit v4 on v3

--- a/solution.py
+++ b/solution.py
@@ -31,7 +31,7 @@
     f_ref, force_ref, sd_ref, sg_ref, rows_ref,
     w_ref, cv_ref, slot_ref, inv_ref, oh_ref, arr_ref, gsend_ref, ghost_ref,
     got_ref, x_ref, add_ref, back_src, back_got, last_src, last_got, gram_src, gram_got,
-    l_sem, gh_send, gh_recv, a_send, a_recv, c_send, z_send, c_recv, b_send, b_recv, r_send, r_recv,
+    l_sem, gh_send, gh_recv, a_send, a_recv, c_send, c_recv, p_recv, b_send, b_recv, r_send, r_recv,
 ):
     ns, nm, nx, slab, ghost, width, slots = sizes
     ny = nm // nx
@@ -159,7 +159,7 @@
         def one(k, _):
             to = (m + k) % nm
             send(arr_ref.at[a, pl.ds(to * slab, slab), :], got_ref.at[buf, m, pl.ds(row * slab, slab), :],
-                 a_send.at[a, to], a_recv.at[a, m], s, to)
+                 a_send, a_recv.at[buf], s, to)
             return 0
 
         lax.fori_loop(1, nm, one, 0)
@@ -169,83 +169,93 @@
     level = (s // 2) % 2
     base, far = level * 2 * pair + c * pair, (1 - level) * 2 * pair + c * pair
     partner, above, below = s + 1 - 2 * c, (s + 2) % ns, (s + ns - 2) % ns
-    leaving = []
 
     def along(a, b):
-        return ((y + a * c + b * (1 - c) + 2 * nx) % ny) * nx + (x + a * (1 - c) + b * c + 2 * nx) % nx
+        return ((y + a * c + b * (1 - c)) % ny) * nx + (x + a * (1 - c) + b * c) % nx
 
     def table(j, first, count=pair):
         return cv_ref.at[j, pl.ds(first, count)]
 
     def post(ref, j, kind, to_s, to_m):
-        sem = c_send.at[len(leaving)]
-        leaving.append((ref, sem))
-        send(ref, ref, sem, c_recv.at[j, kind], to_s, to_m)
+        send(ref, ref, c_send, c_recv.at[kind, j], to_s, to_m)
 
     def await_table(a, b):
         j = along(a, b)
-        arrived(table(j, base), c_recv.at[j, 0])
+        arrived(table(j, base), c_recv.at[0, j])
         return j
 
     def share(j):
         post(table(j, base, pair // 2), j, 1, above, m)
         post(table(j, base + pair // 2, pair // 2), j, 1, below, m)
-        post(table(j, base), j, 2, partner, m)
+        send(table(j, base), table(j, base), c_send, p_recv, partner, m)
 
     def both_ways(j):
         post(table(j, base), j, 0, s, along(0, 1))
-        post(table(j, base), j, 0, s, along(0, -1))
+        post(table(j, base), j, 0, s, along(0, nx - 1))
 
     def fan_first():
         post(table(m, base), m, 0, s, along(1, 0))
-        post(table(m, base), m, 0, s, along(-1, 0))
+        post(table(m, base), m, 0, s, along(nx - 1, 0))
         both_ways(m)
 
-    def pass_first(a):
-        j = await_table(a, 0)
-        post(table(j, base + (0 if a < 0 else pair // 2), pair // 2), j, 0, s, along(-a, 0))
+    def pass_first(i, _):
+        j = await_table(nx - 1 - 2 * i, 0)
+        post(table(j, base + i * (pair // 2), pair // 2), j, 0, s, along(1 + 2 * i, 0))
         both_ways(j)
         share(j)
-
-    def pass_second(a):
-        for b in (-1, 1):
-            j = await_table(a, b)
-            post(table(j, base + (0 if b < 0 else pair // 2), pair // 2), j, 0, s, along(0, -b))
-            share(j)
+        return 0
+
+    def pass_second(a, i):
+        j = await_table(a, nx - 1 - 2 * i)
+        post(table(j, base + i * (pair // 2), pair // 2), j, 0, s, along(0, 1 + 2 * i))
+        share(j)
 
     def tables_one():
-        pass_first(-1)
-        pass_first(1)
-        pass_second(0)
+        lax.fori_loop(0, 2, pass_first, 0)
+
+        def one(i, _):
+            pass_second(0, i)
+            return 0
+
+        lax.fori_loop(0, 2, one, 0)
 
     def tables_two():
         j = await_table(2, 0)
         both_ways(j)
         share(j)
-        pass_second(-1)
-        pass_second(1)
+
+        def one(a, _):
+            def each(i, _):
+                pass_second(nx - 1 - 2 * a, i)
+                return 0
+
+            lax.fori_loop(0, 2, each, 0)
+            return 0
+
+        lax.fori_loop(0, 2, one, 0)
 
     def tables_three():
-        pass_second(2)
-        for a in (0, -1, 1, 2):
+        def one(i, _):
+            pass_second(2, i)
+            return 0
+
+        lax.fori_loop(0, 2, one, 0)
+
+        def last(a, _):
             share(await_table(a, 2))
+            return 0
+
+        lax.fori_loop(0, nx, last, 0)
 
     def tables_other():
         def level_in(k, _):
             j = (m + k) % nm
-            arrived(table(j, far), c_recv.at[j, 1])
-            send(table(j, far), table(j, far), z_send.at[j], c_recv.at[j, 3], partner, m)
+            arrived(table(j, far), c_recv.at[1, j])
+            send(table(j, far), table(j, far), c_send, p_recv, partner, m)
             return 0
 
         lax.fori_loop(1, nm, level_in, 0)
-
-        def core_in(k, _):
-            j = (m + k) % nm
-            arrived(table(j, base + pair - 2 * c * pair), c_recv.at[j, 2])
-            arrived(table(j, far + pair - 2 * c * pair), c_recv.at[j, 3])
-            return 0
-
-        lax.fori_loop(1, nm, core_in, 0)
+        arrived(cv_ref.at[pl.ds(0, nm - 1), pl.ds(0, 2 * pair)], p_recv)
 
     ghosts_out(0)
     loads[2].wait()
@@ -301,14 +311,7 @@
     lanes = 4 * slab
 
     def gather(buf):
-        def one(k, _):
-            j = (m + k) % nm
-            for a in range(7):
-                if PLACE[a][0] == buf:
-                    arrived(got_ref.at[buf, j, pl.ds(PLACE[a][1] * slab, slab), :], a_recv.at[a, j])
-            return 0
-
-        lax.fori_loop(1, nm, one, 0)
+        arrived(got_ref.at[buf, pl.ds(0, nm - 1), pl.ds(0, (3 + buf) * slab), :], a_recv.at[buf])
 
     def turn_x(j, _):
         rows = pl.ds(pl.multiple_of(j * width, width), width)
@@ -358,12 +361,18 @@
 
         @pl.when(odd == 1)
         def _():
-            def turn_back(j, _):
-                block = add_ref[0, pl.ds(pl.multiple_of(j * width, width), width), :]
-                back_src[p // 2, j] = jnp.transpose(block)[lanes - slab :, :]
+            def turn_back(i, _):
+                at = lax.broadcasted_iota(jnp.int32, (width, lanes), 1)
+                packed = add_ref[0, pl.ds(pl.multiple_of((4 * i + 3) * width, width), width), :]
+                for g in range(3):
+                    block = add_ref[0, pl.ds(pl.multiple_of((4 * i + g) * width, width), width), :]
+                    packed = jnp.where((at >= g * slab) & (at < (g + 1) * slab), pltpu.roll(block, (g + 1) * slab, 1), packed)
+                turned = jnp.transpose(packed)
+                for g in range(4):
+                    back_src[p // 2, 4 * i + g] = turned[g * slab : (g + 1) * slab, :]
                 return 0
 
-            lax.fori_loop(0, nm, turn_back, 0, unroll=2)
+            lax.fori_loop(0, nm // 4, turn_back, 0, unroll=2)
 
         @pl.when((p == 1) | (p == 3))
         def _():
@@ -379,7 +388,7 @@
 
         def out(i, _):
             to = (m + i) % nm
-            send(src.at[to], dst.at[m], b_send.at[k, to], b_recv.at[k, m], s, to)
+            send(src.at[to], dst.at[m], b_send.at[k], b_recv.at[k], s, to)
             return 0
 
         lax.fori_loop(1, nm, out, 0)
@@ -397,44 +406,29 @@
 
     def reduce_mode(k, _):
         to = (m + k) % nm
-        send(gram_src.at[0], gram_got.at[0, m], r_send.at[0, to], r_recv.at[0, m], s, to)
+        send(gram_src.at[0], gram_got.at[0, m], r_send.at[0], r_recv.at[0], s, to)
         return 0
 
     lax.fori_loop(1, nm, reduce_mode, 0)
     last_src[...] = back_src[STEPS - 1].astype(BF)
     back_out(STEPS - 1)
 
-    def got_mode(k, _):
-        j = (m + k) % nm
-        arrived(gram_got.at[0, j], r_recv.at[0, j])
-        return 0
-
-    lax.fori_loop(1, nm, got_mode, 0)
+    arrived(gram_got.at[0, pl.ds(0, nm - 1)], r_recv.at[0])
     gram = jnp.sum(gram_got[0, 0:nm], axis=0)
     gram_src[1] = gram
     gram_got[1, s] = gram
 
     def reduce_space(k, _):
         to = (s + k) % ns
-        send(gram_src.at[1], gram_got.at[1, s], r_send.at[1, to], r_recv.at[1, s], to, m)
+        send(gram_src.at[1], gram_got.at[1, s], r_send.at[1], r_recv.at[1], to, m)
         return 0
 
     lax.fori_loop(1, ns, reduce_space, 0)
 
-    def back_in(k, _):
-        j = (m + k) % nm
-        for a in range(STEPS):
-            arrived(back_dst(a, back_got, last_got).at[j], b_recv.at[a, j])
-        return 0
-
-    lax.fori_loop(1, nm, back_in, 0)
-
-    def got_space(k, _):
-        j = (s + k) % ns
-        arrived(gram_got.at[1, j], r_recv.at[1, j])
-        return 0
-
-    lax.fori_loop(1, ns, got_space, 0)
+    for a in range(STEPS):
+        arrived(back_dst(a, back_got, last_got).at[pl.ds(0, nm - 1)], b_recv.at[a])
+
+    arrived(gram_got.at[1, pl.ds(0, ns - 1)], r_recv.at[1])
     total = jnp.sum(jnp.sum(gram_got[1, 0:ns], axis=0), axis=1, keepdims=True) * (1.0 / (nodes * ns * nm * width))
     g00, g01, g11, g02, g12, g22 = [total[r : r + 1, :] for r in range(6)]
 
@@ -453,26 +447,12 @@
     for r in range(3):
         ghosts_sent(r)
 
-    def drain(k, _):
-        to = (m + k) % nm
-        for a in range(7):
-            sent(arr_ref.at[a, pl.ds(to * slab, slab), :], a_send.at[a, to])
-        for a in range(STEPS):
-            sent(back_dst(a, back_src, last_src).at[to], b_send.at[a, to])
-        sent(gram_src.at[0], r_send.at[0, to])
-        sent(table(to, far), z_send.at[to])
-        return 0
-
-    lax.fori_loop(1, nm, drain, 0)
-
-    def drain_space(k, _):
-        sent(gram_src.at[1], r_send.at[1, (s + k) % ns])
-        return 0
-
-    lax.fori_loop(1, ns, drain_space, 0)
-
-    for ref, sem in leaving:
-        sent(ref, sem)
+    sent(arr_ref.at[:, pl.ds(0, (nm - 1) * slab), :], a_send)
+    sent(cv_ref.at[pl.ds(0, nm - 1), pl.ds(0, slots)], c_send)
+    for a in range(STEPS):
+        sent(back_dst(a, back_src, last_src).at[pl.ds(0, nm - 1)], b_send.at[a])
+    sent(gram_got.at[0, pl.ds(0, nm - 1)], r_send.at[0])
+    sent(gram_got.at[1, pl.ds(0, ns - 1)], r_send.at[1])
 
 
 def solution(mesh):
@@ -519,10 +499,10 @@
                 pltpu.VMEM((2, max(nm, ns), 8, width), F32),
                 dma((8,)),
                 dma((3, 2)), dma((3, 2)),
-                dma((7, nm)), dma((7, nm)),
-                dma((72,)), dma((nm,)), dma((nm, 4)),
-                dma((STEPS, nm)), dma((STEPS, nm)),
-                dma((2, max(nm, ns))), dma((2, max(nm, ns))),
+                dma, dma((2,)),
+                dma, dma((2, nm)), dma,
+                dma((STEPS,)), dma((STEPS,)),
+                dma((2,)), dma((2,)),
             ],
             compiler_params=pltpu.CompilerParams(
                 collective_id=0, has_side_effects=True, vmem_limit_bytes=60 * 2**20

time: 77.8 us -> 71.3 us (0.916)
  Pallas kernels: 76 us -> 69.4 us
    pallas_call x1, Pallas kernels: 76 us -> 69.4 us  [step(): pl.pallas_call(functools.partial(kernel, (ns, nm, nx, slab, ghost, width,...]
where the time goes in v4:
time: 71.3 us; the launch traced here: 71.1 us
  Pallas kernels  69.4 us (97%)
  other arithmetic  1.68 us (2%)
    pallas_call x1, Pallas kernels, step(): pl.pallas_call(functools.partial(kernel, (ns, nm, nx, slab, ghost, width,...  69.4 us
    add x1, other arithmetic, step(): return guess + gathered.reshape(nodes, width)  1.68 us

profile of v4, /device:TPU:1, one launch (start us, length us, event | category | flops | bytes accessed | tf_op | source)
XLA Modules:
  0.0 71.1 jit_solution(16169086697140321821)
XLA Ops:
  0.0 0.0 copy-start
  0.0 69.4 %galerkin.1 = f32[16,32,128]{2,1,0:T(8,128)} custom-call(f32[512,128]{1,0:T(8,128)} %f_hbm.1, f32[512,128]{1,0:T(8,128)} %force_hbm.1, bf16[512,512]{1,0:T(8,128)(2,1)} %sd_hbm.1, bf16[512,256]{1,0:T(8,128)(2,1)} %sg_hbm.1, s32[2,128]{1,0:T(2,128)} %rows_hbm.1, bf16[8,128,128]{2,1,0:T(8,128)(2,1)} %vals_hbm.1, s32[8,16]{1,0:T(8,128)} %bitcast.3, ...), custom_call_target="tpu_custom_call" | custom-call | tf_op jit(solution)/shard_map/galerkin/pallas_call | solution.py:472
  69.4 0.0 copy-done
  69.5 1.7 %bitcast_add_fusion = f32[512,128]{1,0:T(8,128)} fusion(f32[512,128]{1,0:T(8,128)S(1)} %copy-done, f32[16,32,128]{2,1,0:T(8,128)} %galerkin.1), kind=kLoop, calls=%fused_computation | loop fusion | flops 65536 | bytes 786432 | tf_op jit(solution)/shard_map/add | solution.py:512
Async XLA Ops:
  0.0 69.4 %copy-start = (f32[512,128]{1,0:T(8,128)S(1)}, f32[512,128]{1,0:T(8,128)}, u32[]{:S(2)}) copy-start(f32[512,128]{1,0:T(8,128)} %f_hbm.1) | copy-start | bytes 786436

commit v5 on v4

--- a/solution.py
+++ b/solution.py
@@ -196,11 +196,11 @@
     def fan_first():
         post(table(m, base), m, 0, s, along(1, 0))
         post(table(m, base), m, 0, s, along(nx - 1, 0))
+        post(table(m, base), m, 0, s, along(2, 0))
         both_ways(m)
 
-    def pass_first(i, _):
-        j = await_table(nx - 1 - 2 * i, 0)
-        post(table(j, base + i * (pair // 2), pair // 2), j, 0, s, along(1 + 2 * i, 0))
+    def pass_first(a, _):
+        j = await_table(a, 0)
         both_ways(j)
         share(j)
         return 0
@@ -211,7 +211,7 @@
         share(j)
 
     def tables_one():
-        lax.fori_loop(0, 2, pass_first, 0)
+        lax.fori_loop(1, nx, pass_first, 0)
 
         def one(i, _):
             pass_second(0, i)
@@ -220,27 +220,17 @@
         lax.fori_loop(0, 2, one, 0)
 
     def tables_two():
-        j = await_table(2, 0)
-        both_ways(j)
-        share(j)
-
         def one(a, _):
             def each(i, _):
-                pass_second(nx - 1 - 2 * a, i)
+                pass_second(a, i)
                 return 0
 
             lax.fori_loop(0, 2, each, 0)
             return 0
 
-        lax.fori_loop(0, 2, one, 0)
+        lax.fori_loop(1, nx, one, 0)
 
     def tables_three():
-        def one(i, _):
-            pass_second(2, i)
-            return 0
-
-        lax.fori_loop(0, 2, one, 0)
-
         def last(a, _):
             share(await_table(a, 2))
             return 0
@@ -255,7 +245,6 @@
             return 0
 
         lax.fori_loop(1, nm, level_in, 0)
-        arrived(cv_ref.at[pl.ds(0, nm - 1), pl.ds(0, 2 * pair)], p_recv)
 
     ghosts_out(0)
     loads[2].wait()
@@ -285,9 +274,9 @@
     ghosts_out(2)
     arr_ref[A_SG] = sg_bf
     arr_ref[A_S2F] = two[:, width : 2 * width]
+    tables_two()
     spread(A_SG)
     spread(A_S2F)
-    tables_two()
     part = dot(sd_ref[...], sg_bf)
     ghosts_in(2)
     arr_ref[A_S2G] = (part + dot(sg_ref[...], ghost_ref[2, :, 0:width])).astype(BF)
@@ -328,9 +317,10 @@
 
     gather(0)
     lax.fori_loop(0, nm, turn_x, 0)
+    tables_other()
     gather(1)
     lax.fori_loop(0, nm, turn_g, 0)
-    tables_other()
+    arrived(cv_ref.at[pl.ds(0, nm - 1), pl.ds(0, 2 * pair)], p_recv)
     table_copy.wait()
 
     def build(t, _):

time: 71.3 us -> 69.9 us (0.980)
  Pallas kernels: 69.4 us -> 68 us
    pallas_call x1, Pallas kernels: 69.4 us -> 68 us  [step(): pl.pallas_call(functools.partial(kernel, (ns, nm, nx, slab, ghost, width,...]
where the time goes in v5:
time: 69.9 us; the launch traced here: 69.7 us
  Pallas kernels  68 us (97%)
  other arithmetic  1.68 us (2%)
    pallas_call x1, Pallas kernels, step(): pl.pallas_call(functools.partial(kernel, (ns, nm, nx, slab, ghost, width,...  68 us
    add x1, other arithmetic, step(): return guess + gathered.reshape(nodes, width)  1.68 us

profile of v5, /device:TPU:1, one launch (start us, length us, event | category | flops | bytes accessed | tf_op | source)
XLA Modules:
  0.0 69.7 jit_solution(4134240155632983825)
XLA Ops:
  0.0 0.0 copy-start
  0.0 68.0 %galerkin.1 = f32[16,32,128]{2,1,0:T(8,128)} custom-call(f32[512,128]{1,0:T(8,128)} %f_hbm.1, f32[512,128]{1,0:T(8,128)} %force_hbm.1, bf16[512,512]{1,0:T(8,128)(2,1)} %sd_hbm.1, bf16[512,256]{1,0:T(8,128)(2,1)} %sg_hbm.1, s32[2,128]{1,0:T(2,128)} %rows_hbm.1, bf16[8,128,128]{2,1,0:T(8,128)(2,1)} %vals_hbm.1, s32[8,16]{1,0:T(8,128)} %bitcast.3, ...), custom_call_target="tpu_custom_call" | custom-call | tf_op jit(solution)/shard_map/galerkin/pallas_call | solution.py:462
  68.0 0.0 copy-done
  68.1 1.7 %bitcast_add_fusion = f32[512,128]{1,0:T(8,128)} fusion(f32[512,128]{1,0:T(8,128)S(1)} %copy-done, f32[16,32,128]{2,1,0:T(8,128)} %galerkin.1), kind=kLoop, calls=%fused_computation | loop fusion | flops 65536 | bytes 786432 | tf_op jit(solution)/shard_map/add | solution.py:502
Async XLA Ops:
  0.0 68.0 %copy-start = (f32[512,128]{1,0:T(8,128)S(1)}, f32[512,128]{1,0:T(8,128)}, u32[]{:S(2)}) copy-start(f32[512,128]{1,0:T(8,128)} %f_hbm.1) | copy-start | bytes 786436

commit v6 on v5

--- a/solution.py
+++ b/solution.py
@@ -316,10 +316,10 @@
         return 0
 
     gather(0)
-    lax.fori_loop(0, nm, turn_x, 0)
+    lax.fori_loop(0, nm, turn_x, 0, unroll=4)
     tables_other()
     gather(1)
-    lax.fori_loop(0, nm, turn_g, 0)
+    lax.fori_loop(0, nm, turn_g, 0, unroll=4)
     arrived(cv_ref.at[pl.ds(0, nm - 1), pl.ds(0, 2 * pair)], p_recv)
     table_copy.wait()
 
@@ -328,7 +328,7 @@
             w_ref[0, pl.ds(pl.multiple_of(t * width, width), width), j * width : (j + 1) * width] = cv_ref[j, inv_ref[t, j]]
         return 0
 
-    lax.fori_loop(0, nm, build, 0)
+    lax.fori_loop(0, nm, build, 0, unroll=2)
     loads[6].wait()
 
     rows_at_once = nm * width // 2
@@ -362,7 +362,7 @@
                     back_src[p // 2, 4 * i + g] = turned[g * slab : (g + 1) * slab, :]
                 return 0
 
-            lax.fori_loop(0, nm // 4, turn_back, 0, unroll=2)
+            lax.fori_loop(0, nm // 4, turn_back, 0, unroll=4)
 
         @pl.when((p == 1) | (p == 3))
         def _():

time: 69.9 us -> 67.8 us (0.970)
  Pallas kernels: 68 us -> 66 us
    pallas_call x1, Pallas kernels: 68 us -> 66 us  [step(): pl.pallas_call(functools.partial(kernel, (ns, nm, nx, slab, ghost, width,...]
where the time goes in v6:
time: 67.8 us; the launch traced here: 67.7 us
  Pallas kernels  66 us (97%)
  other arithmetic  1.68 us (2%)
    pallas_call x1, Pallas kernels, step(): pl.pallas_call(functools.partial(kernel, (ns, nm, nx, slab, ghost, width,...  66 us
    add x1, other arithmetic, step(): return guess + gathered.reshape(nodes, width)  1.68 us

profile of v6, /device:TPU:1, one launch (start us, length us, event | category | flops | bytes accessed | tf_op | source)
XLA Modules:
  0.0 67.7 jit_solution(3591020927343003050)
XLA Ops:
  0.0 0.0 copy-start
  0.0 66.0 %galerkin.1 = f32[16,32,128]{2,1,0:T(8,128)} custom-call(f32[512,128]{1,0:T(8,128)} %f_hbm.1, f32[512,128]{1,0:T(8,128)} %force_hbm.1, bf16[512,512]{1,0:T(8,128)(2,1)} %sd_hbm.1, bf16[512,256]{1,0:T(8,128)(2,1)} %sg_hbm.1, s32[2,128]{1,0:T(2,128)} %rows_hbm.1, bf16[8,128,128]{2,1,0:T(8,128)(2,1)} %vals_hbm.1, s32[8,16]{1,0:T(8,128)} %bitcast.3, ...), custom_call_target="tpu_custom_call" | custom-call | tf_op jit(solution)/shard_map/galerkin/pallas_call | solution.py:462
  66.0 0.0 copy-done
  66.0 1.7 %bitcast_add_fusion = f32[512,128]{1,0:T(8,128)} fusion(f32[512,128]{1,0:T(8,128)S(1)} %copy-done, f32[16,32,128]{2,1,0:T(8,128)} %galerkin.1), kind=kLoop, calls=%fused_computation | loop fusion | flops 65536 | bytes 786432 | tf_op jit(solution)/shard_map/add | solution.py:502
Async XLA Ops:
  0.0 66.0 %copy-start = (f32[512,128]{1,0:T(8,128)S(1)}, f32[512,128]{1,0:T(8,128)}, u32[]{:S(2)}) copy-start(f32[512,128]{1,0:T(8,128)} %f_hbm.1) | copy-start | bytes 786436
